TPU v7x, 32 devices: a whole 2x2x4 slice. The times are simulated.
32 devices in a mesh: ifg: 8 (over y, x, core), row: 4 (over z).
Axes of the slice: x: 2, y: 2, z: 4, core: 2. Of those that a mesh axis runs over, the one named last changes fastest.
Arguments:
- ifg_real: bfloat16 [256, 256, 512], P('ifg', 'row'), may hold values from -6 to 6
- ifg_imag: bfloat16 [256, 256, 512], P('ifg', 'row'), may hold values from -6 to 6
- date_pairs: int32 [256, 2], replicated, may hold values from 0 to 319, as said below
Outputs:
- corrected: float32 [320, 256, 512], P('ifg', 'row')
- atmosphere: float32 [320, 256, 512], P('ifg', 'row')
Inputs may be any that keep to these rules, and one draw needn't show every extreme that they name: `date_pairs`: each row holds a reference date and a later secondary date, 1 to 5 dates apart.
All inputs are finite; a program needn't handle non-finite values.
Results may differ from a plain program's by a relative error of at most 0.0078.
Values may be sent and summed in bfloat16 or wider, within the bound.
A program may use at most 128 MiB of HBM per device.

v0:
```python
import math

import jax
import jax.numpy as jnp
from jax import lax
from jax.sharding import PartitionSpec as P

PATCH = 64
NDATES = 320
ITERS = 3
RADIUS = 16


goldstein_power = 0.5
huber_threshold = 0.3
blur_sigma = 5.0
ridge_weight = 1.0


def padded_2(block, sides, width):
    for axis, dim in sides:
        count = lax.axis_size(axis)
        forward = [(i, i + 1) for i in range(count - 1)]
        backward = [(target, source) for source, target in forward]
        low = lax.ppermute(
            lax.slice_in_dim(block, block.shape[dim] - width, None, axis=dim), axis, forward
        )
        high = lax.ppermute(lax.slice_in_dim(block, 0, width, axis=dim), axis, backward)
        block = jnp.concatenate([low, block, high], axis=dim)
    return block


def spectral_tables():
    counter = jnp.arange(PATCH, dtype=jnp.int32)
    phase_steps = counter[:, None] * counter[None, :] % PATCH
    angles = phase_steps.astype(jnp.float32) * (2.0 * math.pi / PATCH)
    scaling = 1.0 / math.sqrt(PATCH)
    cosine = jnp.cos(angles) * scaling
    sine_lookup = jnp.sin(angles) * scaling
    forward = jnp.concatenate(
        [jnp.concatenate([cosine, -sine_lookup], 1), jnp.concatenate([sine_lookup, cosine], 1)], 0
    )
    inverse = jnp.concatenate(
        [jnp.concatenate([cosine, sine_lookup], 1), jnp.concatenate([-sine_lookup, cosine], 1)], 0
    )
    taper_row = jnp.sin(math.pi * (jnp.arange(PATCH, dtype=jnp.float32) + 0.5) / PATCH) ** 2
    return (
        forward.astype(jnp.bfloat16),
        inverse.astype(jnp.bfloat16),
        cosine.astype(jnp.bfloat16),
        sine_lookup.astype(jnp.bfloat16),
        taper_row,
    )


def row_apply(values, cosine, sine_lookup, direction):
    flipped = jnp.concatenate([values[..., PATCH:], -values[..., :PATCH]], axis=-1)
    first = jnp.einsum("kb,anbcl->ankcl", cosine, values, preferred_element_type=jnp.float32)
    second = jnp.einsum("kb,anbcl->ankcl", sine_lookup, flipped, preferred_element_type=jnp.float32)
    return first + direction * second


def filter_block(padded, tables):
    forward, inverse, cosine, sine_lookup, taper_row = tables
    block_count = padded.shape[0]
    rows_pad = padded.shape[2]
    cols_pad = padded.shape[3]
    half_patch = PATCH // 2
    taper_both = jnp.concatenate([taper_row, taper_row])
    canvas = jnp.zeros((block_count, 2, rows_pad, cols_pad), jnp.float32)
    for row_shift in (0, half_patch):
        for col_shift in (0, half_patch):
            window = padded[
                :, :, row_shift : rows_pad - row_shift, col_shift : cols_pad - col_shift
            ]
            row_tiles = window.shape[2] // PATCH
            col_tiles = window.shape[3] // PATCH
            tile_grid = window.reshape(block_count, 2, row_tiles, PATCH, col_tiles, PATCH)
            stacked = jnp.concatenate([tile_grid[:, 0], tile_grid[:, 1]], axis=-1)
            column_spectra = jnp.einsum(
                "anbcl,lm->anbcm", stacked, forward, preferred_element_type=jnp.float32
            ).astype(jnp.bfloat16)
            spectra = row_apply(column_spectra, cosine, sine_lookup, 1.0)
            spectral_power = spectra[..., :PATCH] ** 2 + spectra[..., PATCH:] ** 2 + 1.0
            shaping = spectral_power ** (0.5 * goldstein_power)
            shaped = (spectra * jnp.concatenate([shaping, shaping], axis=-1)).astype(jnp.bfloat16)
            row_back = row_apply(shaped, cosine, sine_lookup, -1.0).astype(jnp.bfloat16)
            restored = jnp.einsum(
                "anbcl,lm->anbcm", row_back, inverse, preferred_element_type=jnp.float32
            )
            weighted = restored * taper_row[:, None, None] * taper_both
            pieces = jnp.stack([weighted[..., :PATCH], weighted[..., PATCH:]], axis=1)
            pieces = pieces.reshape(block_count, 2, row_tiles * PATCH, col_tiles * PATCH)
            canvas = canvas + jnp.pad(
                pieces, ((0, 0), (0, 0), (row_shift, row_shift), (col_shift, col_shift))
            )
    return canvas[:, :, half_patch : rows_pad - half_patch, half_patch : cols_pad - half_patch]


def sine_of(real_part, imag_part):
    real_wide = real_part.astype(jnp.float32)
    imag_wide = imag_part.astype(jnp.float32)
    return (imag_wide / jnp.sqrt(real_wide * real_wide + imag_wide * imag_wide + 1.0)).astype(
        jnp.bfloat16
    )


def projection(date_pairs):
    date_index = jnp.arange(NDATES, dtype=jnp.int32)
    design = (date_pairs[:, 1:2] == date_index[None, :]).astype(jnp.float32) - (
        date_pairs[:, 0:1] == date_index[None, :]
    ).astype(jnp.float32)
    gram = jnp.dot(design.T, design, precision=lax.Precision.HIGHEST) + ridge_weight * jnp.eye(
        NDATES, dtype=jnp.float32
    )
    cholesky_factor = jnp.linalg.cholesky(gram)
    halfway = lax.linalg.triangular_solve(cholesky_factor, design.T, left_side=True, lower=True)
    mapping = lax.linalg.triangular_solve(
        cholesky_factor, halfway, left_side=True, lower=True, transpose_a=True
    )
    return (design, mapping)


def invert_rows(phase_sines, design, mapping):
    total_ifg = phase_sines.shape[0]
    row_count = phase_sines.shape[1]
    strip_cols = phase_sines.shape[2]
    observed = phase_sines.reshape(total_ifg, row_count * strip_cols).astype(jnp.float32)
    series = jnp.zeros((NDATES, observed.shape[1]), jnp.float32)
    misfit = observed
    for iteration in range(ITERS):
        if iteration > 0:
            misfit = observed - jnp.dot(design, series, precision=lax.Precision.HIGHEST)
        series = series + jnp.dot(
            mapping,
            jnp.clip(misfit, -huber_threshold, huber_threshold),
            precision=lax.Precision.HIGHEST,
        )
    return series.reshape(NDATES, row_count, strip_cols)


def gauss_matrix(size_out, size_in, offset):
    out_index = jnp.arange(size_out, dtype=jnp.int32)[:, None]
    in_index = jnp.arange(size_in, dtype=jnp.int32)[None, :]
    distance = in_index - offset - out_index
    kernel = jnp.exp(-0.5 * (distance.astype(jnp.float32) / blur_sigma) ** 2)
    return jnp.where(jnp.abs(distance) <= RADIUS, kernel, 0.0)


def row_weights(row_filter_kernel, local_rows):
    total_rows = local_rows * lax.axis_size("row")
    source_rows = (
        lax.axis_index("row") * local_rows
        - RADIUS
        + jnp.arange(local_rows + 2 * RADIUS, dtype=jnp.int32)
    )
    inside = (source_rows >= 0) & (source_rows < total_rows)
    return jnp.sum(jnp.where(inside[None, :], row_filter_kernel, 0.0), axis=1)


def on_device(ifg_real, ifg_imag, date_pairs):
    tables = spectral_tables()
    half_patch = PATCH // 2
    local_count = ifg_real.shape[0]
    local_rows = ifg_real.shape[1]
    width_cols = ifg_real.shape[2]
    joined = jnp.stack([ifg_real, ifg_imag], axis=1)
    extended = padded_2(joined, (("row", 2),), half_patch)
    padded = jnp.pad(extended, ((0, 0), (0, 0), (0, 0), (half_patch, half_patch)))
    block_list = padded.reshape(local_count // 2, 2, 2, local_rows + PATCH, width_cols + PATCH)

    def run_block(block_data):
        return filter_block(block_data, tables).astype(jnp.bfloat16)

    filtered = lax.map(run_block, block_list).reshape(local_count, 2, local_rows, width_cols)
    design, mapping = projection(date_pairs)
    local_sines = sine_of(filtered[:, 0], filtered[:, 1])
    series = invert_rows(
        lax.all_to_all(local_sines, "ifg", split_axis=2, concat_axis=0, tiled=True), design, mapping
    )
    row_filter_kernel = gauss_matrix(local_rows, local_rows + 2 * RADIUS, RADIUS)
    row_weight = row_weights(row_filter_kernel, local_rows)
    col_kernel = gauss_matrix(width_cols, width_cols, 0)
    values = lax.all_to_all(series, "ifg", split_axis=0, concat_axis=2, tiled=True)
    smoothed_columns = jnp.einsum(
        "drc,ce->dre", values, col_kernel, precision=lax.Precision.HIGHEST
    )
    with_borders = padded_2(smoothed_columns, (("row", 1),), RADIUS)
    smoothed_phase = jnp.einsum(
        "om,nmb->nob", row_filter_kernel, with_borders, precision=lax.Precision.HIGHEST
    )
    weight = row_weight[:, None] * jnp.sum(col_kernel, axis=0)[None, :]
    atmosphere = smoothed_phase / weight
    return (values - atmosphere, atmosphere)


def solution(mesh):
    placed = (P("ifg", "row", None), P("ifg", "row", None), P())
    return jax.shard_map(
        on_device,
        mesh=mesh,
        in_specs=placed,
        out_specs=(P("ifg", "row", None), P("ifg", "row", None)),
        check_vma=False,
    )
```

profile of v0, /device:TPU:0, one launch (start us, length us, event | category | flops | bytes accessed | tf_op | source)
XLA Modules:
  0.0 1257.0 jit_solution(8156905076809823349)
XLA Ops:
  0.6 5.0 copy.124
  5.6 3.1 copy.125
  8.7 14.1 %slice_maximum_fusion = (bf16[32,2,32,512]{2,3,1,0:T(8,128)(2,1)}, bf16[32,2,32,512]{2,3,1,0:T(8,128)(2,1)}) fusion(bf16[32,1,64,512]{2,3,1,0:T(8,128)(2,1)} %bitcast.406, bf16[32,1,64,512]{2,3,1,0:T(8,128)(2,1)} %bitcast.404), kind=kLoop, calls=%fused_computation.296 | loop fusion | flops 8388608 | bytes 8388608 | tf_op jit(solution)/shard_map/stack | solution.py:167
  22.8 6.7 copy.126
  29.5 6.3 collective-permute-start
  35.9 8.0 copy.127
  47.7 11.7 cholesky.78
  59.4 9.8 custom-call.24
  71.6 11.7 cholesky.164
  83.3 10.4 custom-call.25
  94.9 5.8 cholesky.186
  104.2 3.8 while.15
  108.1 29.5 %custom-call.26 = f32[3,128,128]{1,2,0:T(8,128)S(1)} custom-call(f32[3,128,128]{2,1,0:T(8,128)S(1)} %pad_maximum_fusion.4), custom_call_target="InvertDiagBlocksLowerTriangular" | custom-call | tf_op jit(solution)/shard_map/triangular_solve | solution.py:118
  140.1 7.8 copy.128
  147.9 7.8 copy.129
  155.6 17.2 %select_maximum_fusion = bf16[32,2,128,576]{2,3,1,0:T(8,128)(2,1)} fusion(bf16[32,2,32,512]{2,3,1,0:T(8,128)(2,1)} %copy.129, bf16[32,2,32,512]{2,3,1,0:T(8,128)(2,1)} %copy.128, bf16[32,1,64,512]{2,3,1,0:T(8,128)(2,1)} %bitcast.407, bf16[32,1,64,512]{2,3,1,0:T(8,128)(2,1)} %bitcast.405), kind=kLoop, calls=%fused_computation.290 | loop fusion | flops 70778880 | bytes 17825792 | tf_op jit(solution)/shard_map/concatenate | solution.py:29
  172.8 760.5 %while.16 = (s32[]{:T(128)}, bf16[16,2,2,64,512]{4,3,2,1,0:T(8,128)(2,1)}, bf16[16,2,2,128,576]{3,4,2,1,0:T(8,128)(2,1)}, bf16[128,128]{1,0:T(8,128)(2,1)}, bf16...) while((s32[]{:T(128)}, bf16[16,2,2,64,512]{4,3,2,1,0:T(8,128)(2,1)}, ...), condition=%wide.region_7.8_spmd.clone.clone, body=%wide.region_6.7_spmd.clone.clone.sunk | while | flops 882688192 | bytes 94506920 | solution.py:175
  210.0 2.1 copy.201
  214.5 4.0 fusion.539
  262.0 4.0 fusion.539
  305.0 2.1 copy.201
  309.5 4.0 fusion.539
  357.0 4.0 fusion.539
  404.5 4.0 fusion.539
  452.0 4.0 fusion.539
  499.5 4.0 fusion.539
  547.0 4.0 fusion.539
  594.5 4.0 fusion.539
  642.0 4.0 fusion.539
  689.5 4.0 fusion.539
  737.0 4.0 fusion.539
  784.5 4.0 fusion.539
  832.0 4.0 fusion.539
  879.5 4.0 fusion.539
  927.0 4.0 fusion.539
  933.3 3.4 fusion.254
  936.7 6.6 copy.132
  943.3 7.6 reshape.362
  950.9 3.7 all-to-all-start
  959.5 21.7 %all-to-all-done = bf16[8,2,65536]{2,1,0:T(2,128)(2,1)S(1)} async-done(((bf16[8,2,65536]{2,1,0:T(2,128)(2,1)}), bf16[8,2,65536]{2,1,0:T(2,128)(2,1)S(1)}, u32[]{:S(2)}, u32[]{:S(2)}) %all-to-all-start) | async-done | bytes 2097184 | tf_op jit(solution)/shard_map/all_to_all | solution.py:179
  981.3 4.9 reshape.363
  986.2 4.5 copy.133
  990.7 4.2 reshape.337
  994.9 8.2 copy.134
  1003.1 7.9 reshape.336
  1011.0 6.8 fusion.255
  1017.8 7.4 fusion.249
  1025.2 5.1 convolution_add_fusion.6
  1030.3 7.6 fusion.250
  1037.9 6.3 convolution_add_fusion.5
  1044.2 6.3 copy.135
  1050.5 12.4 copy.136
  1062.9 11.2 reshape.364
  1074.1 64.8 %all_to_all.27 = f32[8,1,163840]{2,1,0:T(1,128)} all-to-all(f32[8,1,163840]{2,1,0:T(1,128)} %reshape.364), channel_id=1, replica_groups=mesh['ifg'=8,'row'=4] {'ifg'}, dimensions={0} | all-to-all | bytes 10485760 | tf_op jit(solution)/shard_map/all_to_all | solution.py:184
  1139.4 17.0 %reduce.18 = f32[8,163840]{1,0:T(8,128)} reduce(f32[8,1,163840]{2,1,0:T(1,128)} %all_to_all.27, f32[]{:T(128)} %broadcast.601), dimensions={1}, to_apply=%all_to_all.21.reduce_sub_computation | reduce | bytes 10485764 | tf_op jit(solution)/shard_map/all_to_all | solution.py:184
  1156.5 10.6 reshape.365
  1167.0 17.8 %copy.137 = f32[40,64,8,64]{3,2,1,0:T(8,128)} copy(f32[40,64,8,64]{3,1,0,2:T(8,128)} %bitcast.403) | data formatting | bytes 10485760 | tf_op jit(solution)/shard_map/all_to_all | solution.py:184
  1184.9 9.4 all_to_all.24
  1194.3 11.2 fusion.261
  1205.5 2.3 copy-done.4
  1208.1 5.6 collective-permute-start.2
  1215.4 24.7 %collective-permute-done.2 = f32[40,16,512]{2,1,0:T(8,128)} collective-permute-done((f32[40,16,512]{2,1,0:T(8,128)S(1)}, f32[40,16,512]{2,1,0:T(8,128)}, u32[]{:S(2)}, u32[]{:S(2)}) %collective-permute-start.2) | collective-permute-done | bytes 1310752 | tf_op jit(solution)/shard_map/ppermute | solution.py:25
  1240.1 5.3 collective-permute-done.3
  1245.4 11.5 fusion.351
  (1464 shorter events, 706.4 us)
Async XLA Ops:
  0.6 5.0 copy-start.6
  29.5 110.5 %collective-permute-start = (bf16[32,2,32,512]{3,2,1,0:T(8,128)(2,1)S(1)}, bf16[32,2,32,512]{3,2,1,0:T(8,128)(2,1)}, u32[]{:S(2)}, u32[]{:S(2)}) collective-permute-start(bf16[32,2,32,512]{3,2,1,0:T(8,128)(2,1)S(1)} %copy.126), channel_id=1, source_target_pairs={{0,1},{1,2},{2,3},{4,5},{5,6},{6,7},{8,9},{9,10},{10,11},{12,13},{... | collective-permute-start | bytes 6291464 | tf_op jit(solution)/shard_map/ppermute | solution.py:25
  35.9 9.6 copy-start.18
  43.9 103.9 %collective-permute-start.1 = (bf16[32,2,32,512]{3,2,1,0:T(8,128)(2,1)}, bf16[32,2,32,512]{3,2,1,0:T(8,128)(2,1)}, u32[]{:S(2)}, u32[]{:S(2)}) collective-permute-start(bf16[32,2,32,512]{3,2,1,0:T(8,128)(2,1)} %copy.127), channel_id=1, source_target_pairs={{1,0},{2,1},{3,2},{5,4},{6,5},{7,6},{9,8},{10,9},{11,10},{13,12},{... | collective-permute-start | bytes 6291464 | tf_op jit(solution)/shard_map/ppermute | solution.py:28
  45.5 93.6 %copy-start.14 = (s32[256,1]{0,1:T(1,128)}, s32[256,1]{0,1:T(1,128)S(1)}, u32[]{:S(2)}) copy-start(s32[256,1]{0,1:T(1,128)S(1)} %get-tuple-element.298) | copy-start | bytes 3076
  45.5 93.6 %copy-start.16 = (s32[256,1]{0,1:T(1,128)}, s32[256,1]{0,1:T(1,128)S(1)}, u32[]{:S(2)}) copy-start(s32[256,1]{0,1:T(1,128)S(1)} %get-tuple-element.299) | copy-start | bytes 3076
  108.0 39.8 %copy-start.5 = (f32[320,320]{1,0:T(8,128)}, f32[320,320]{1,0:T(8,128)S(1)}, u32[]{:S(2)}) copy-start(f32[320,320]{1,0:T(8,128)S(1)} %get-tuple-element.485) | copy-start | bytes 1228804
  137.6 10.3 copy-start.11
  138.8 9.0 copy-start.9
  139.1 8.7 copy-start.7
  191.8 1.5 copy-start.3
  207.8 6.7 copy-start.1
  207.8 6.7 copy-start.2
  239.3 1.5 copy-start.3
  255.3 6.7 copy-start.1
  255.3 6.7 copy-start.2
  286.8 1.5 copy-start.3
  302.8 6.7 copy-start.1
  302.8 6.7 copy-start.2
  334.3 1.5 copy-start.3
  350.3 6.7 copy-start.1
  350.3 6.7 copy-start.2
  381.8 1.5 copy-start.3
  397.8 6.7 copy-start.1
  397.8 6.7 copy-start.2
  429.3 1.5 copy-start.3
  445.3 6.7 copy-start.1
  445.3 6.7 copy-start.2
  476.8 1.5 copy-start.3
  492.8 6.7 copy-start.1
  492.8 6.7 copy-start.2
  524.3 1.5 copy-start.3
  540.3 6.7 copy-start.1
  540.3 6.7 copy-start.2
  571.8 1.5 copy-start.3
  587.8 6.7 copy-start.1
  587.8 6.7 copy-start.2
  619.3 1.5 copy-start.3
  635.3 6.7 copy-start.1
  635.3 6.7 copy-start.2
  666.8 1.5 copy-start.3
  682.8 6.7 copy-start.1
  682.8 6.7 copy-start.2
  714.3 1.5 copy-start.3
  730.3 6.7 copy-start.1
  730.3 6.7 copy-start.2
  777.8 6.7 copy-start.1
  777.8 6.7 copy-start.2
  825.3 6.7 copy-start.1
  825.3 6.7 copy-start.2
  872.8 6.7 copy-start.1
  872.8 6.7 copy-start.2
  920.3 6.7 copy-start.1
  920.3 6.7 copy-start.2
  943.3 11.3 copy-start.12
  943.3 11.4 copy-start.13
  943.3 11.7 copy-start.8
  950.9 30.3 %all-to-all-start = ((bf16[8,2,65536]{2,1,0:T(2,128)(2,1)}), bf16[8,2,65536]{2,1,0:T(2,128)(2,1)S(1)}, u32[]{:S(2)}, u32[]{:S(2)}) async-start(bf16[8,2,65536]{2,1,0:T(2,128)(2,1)} %reshape.362), calls=%async_computation | async-start | bytes 4194304 | tf_op jit(solution)/shard_map/all_to_all | solution.py:179
  1011.0 6.8 copy-start
  1011.0 6.8 copy-start.15
  1011.0 6.8 copy-start.17
  1205.5 2.3 copy-start.4
  1208.1 32.0 %collective-permute-start.2 = (f32[40,16,512]{2,1,0:T(8,128)S(1)}, f32[40,16,512]{2,1,0:T(8,128)}, u32[]{:S(2)}, u32[]{:S(2)}) collective-permute-start(f32[40,16,512]{2,1,0:T(8,128)S(1)} %get-tuple-element.287), channel_id=1, source_target_pairs={{0,1},{1,2},{2,3},{4,5},{5,6},{6,7},{8,9},{9,10},{10,11},{12,13},{... | collective-permute-start | bytes 3932168 | tf_op jit(solution)/shard_map/ppermute | solution.py:25
  1213.7 31.7 %collective-permute-start.3 = (f32[40,16,512]{2,1,0:T(8,128)S(1)}, f32[40,16,512]{2,1,0:T(8,128)}, u32[]{:S(2)}, u32[]{:S(2)}) collective-permute-start(f32[40,16,512]{2,1,0:T(8,128)S(1)} %get-tuple-element.288), channel_id=1, source_target_pairs={{1,0},{2,1},{3,2},{5,4},{6,5},{7,6},{9,8},{10,9},{11,10},{13,12},{... | collective-permute-start | bytes 3932168 | tf_op jit(solution)/shard_map/ppermute | solution.py:28
  (5 other events, 7.0 us)
where the time goes:
time: 1270 us; the launch traced here: 1260 us
  local copies, waits for them, and re-layouts  552 us (43%)
  other arithmetic  282 us (22%)
  matrix products  275 us (22%)
  blocking collectives  64.8 us (5%)
  waiting for transfers between devices  51.7 us (4%)
  starting transfers between devices  18.5 us (1%)
    another operation x128, local copies, waits for them, and re-layouts, filter_block(): pieces = jnp.stack([weighted[..., :PATCH], weighted[..., PATCH:]], axis=1)  157 us
    dot_general x64, matrix products, filter_block(): jnp.einsum('anbcl,lm->anbcm', stacked, forward, preferred_element_type=jn...  71.1 us
    all_to_all x1, blocking collectives, on_device(): lax.all_to_all(series, 'ifg', split_axis=0, concat_axis=2, tiled=True)  64.8 us
    broadcast_in_dim x17, other arithmetic, on_device(): lax.map(run_block, block_list)  63.7 us
    slice x128, local copies, waits for them, and re-layouts, filter_block(): pieces = jnp.stack([weighted[..., :PATCH], weighted[..., PATCH:]], axis=1)  61.9 us
    another operation x10, other arithmetic, projection(): cholesky_factor = jnp.linalg.cholesky(gram)  50.9 us
    dot_general x128, matrix products, row_apply(): jnp.einsum('kb,anbcl->ankcl', cosine, values, preferred_element_type=jnp....  47 us
    dot_general x64, matrix products, filter_block(): jnp.einsum('anbcl,lm->anbcm', row_back, inverse, preferred_element_type=j...  45.9 us
  transfers between devices with their start and end apart: 5, of which 3 were waited for; matrix products, arithmetic and copies ran while one was open for 9% of the time, Pallas kernels for 0%

commit v1 on v0

v1 whole, which is shorter than its diff:
```python
import functools
import math

import jax
import jax.numpy as jnp
import numpy as np
from jax import lax
from jax.experimental import pallas as pl
from jax.experimental.pallas import tpu as pltpu
from jax.sharding import PartitionSpec as P

PATCH = 64
HALF = PATCH // 2
RADIUS = 16
NDATES = 320
ITERS = 3

huber_threshold = 0.3
blur_sigma = 5.0

BF = jnp.bfloat16
F32 = jnp.float32
CHUNKS = 2


def mm(a, b):
    return jnp.dot(a, b, preferred_element_type=F32)


def split2(x):
    high = x.astype(BF)
    return high, (x - high.astype(F32)).astype(BF)


def split3(x):
    high = x.astype(BF)
    rest = x - high.astype(F32)
    mid = rest.astype(BF)
    return high, mid, (rest - mid.astype(F32)).astype(BF)


def mm3(a, b):
    ah, al = split2(a)
    bh, bl = split2(b)
    return mm(ah, bh) + (mm(ah, bl) + mm(al, bh))


def spectral_tables(local_rows):
    k = np.arange(PATCH)
    angles = ((k[:, None] * k[None, :]) % PATCH).astype(np.float32) * np.float32(
        2.0 * math.pi / PATCH
    )
    scaling = np.float32(1.0 / math.sqrt(PATCH))
    rounded = lambda v: np.asarray(v.astype(np.float32)).astype(BF).astype(np.float32)
    c = rounded(np.cos(angles) * scaling)
    s = rounded(np.sin(angles) * scaling)
    taper = (
        np.sin(np.float32(math.pi) * (k.astype(np.float32) + np.float32(0.5)) / PATCH) ** 2
    ).astype(np.float32)
    two = np.eye(2, dtype=np.float32)
    cc, ss = np.kron(two, c), np.kron(two, s)
    col_forward = np.block([[cc, -ss], [ss, cc]])
    col_inverse = np.block([[cc, ss], [-ss, cc]])
    extended = local_rows + PATCH
    starts = list(range(0, extended - PATCH + 1, HALF))
    count = len(starts)
    row_forward = np.zeros((2, count, PATCH, 2, extended), np.float32)
    row_inverse = np.zeros((2, extended, 2, count, PATCH), np.float32)
    for p, at in enumerate(starts):
        where = slice(at, at + PATCH)
        row_forward[0, p, :, 0, where] = c
        row_forward[0, p, :, 1, where] = s
        row_forward[1, p, :, 0, where] = -s
        row_forward[1, p, :, 1, where] = c
        tc, ts = taper[:, None] * c, taper[:, None] * s
        row_inverse[0, where, 0, p, :] = tc
        row_inverse[0, where, 1, p, :] = -ts
        row_inverse[1, where, 0, p, :] = ts
        row_inverse[1, where, 1, p, :] = tc
    row_forward = row_forward.reshape(2 * count * PATCH, 2 * extended)
    row_inverse = row_inverse[:, HALF : HALF + local_rows].reshape(
        2 * local_rows, 2 * count * PATCH
    )
    return (
        jnp.asarray(col_forward.astype(BF)),
        jnp.asarray(row_forward.astype(BF)),
        jnp.asarray(row_inverse.astype(BF)),
        jnp.asarray(col_inverse.astype(BF)),
        jnp.asarray(np.tile(taper, 4)[None, :]),
    )


def filter_kernel(re, im, low_re, low_im, high_re, high_im, cf, rf, ri, ci, tp, out, *scratch):
    pad_re, pad_im, even_re, even_im, odd_re, odd_im = scratch
    group, rows, cols = re.shape
    extended = rows + PATCH
    wide = pad_re.shape[1]
    even_tiles = cols // 128
    odd_tiles = wide // 128
    tiles = even_tiles + odd_tiles
    half = rf.shape[0] // 2

    @pl.when(pl.program_id(0) == 0)
    def _():
        pad_re[...] = jnp.zeros_like(pad_re)
        pad_im[...] = jnp.zeros_like(pad_im)

    def one(i, carry):
        x_re = jnp.concatenate([low_re[i], re[i], high_re[i]], axis=0)
        x_im = jnp.concatenate([low_im[i], im[i], high_im[i]], axis=0)
        pad_re[:, HALF : HALF + cols] = x_re
        pad_im[:, HALF : HALF + cols] = x_im

        def tile_of(t):
            if t < even_tiles:
                at = slice(128 * t, 128 * t + 128)
                return jnp.concatenate([x_re[:, at], x_im[:, at]], axis=1)
            at = slice(128 * (t - even_tiles), 128 * (t - even_tiles) + 128)
            return jnp.concatenate([pad_re[:, at], pad_im[:, at]], axis=1)

        for first in range(0, tiles, 2):
            members = list(range(first, min(first + 2, tiles)))
            stacked = jnp.concatenate([tile_of(t) for t in members], axis=0)
            y = mm(stacked, cf[...]).astype(BF)
            parts = []
            for n in range(len(members)):
                piece = y[n * extended : (n + 1) * extended]
                parts.append(jnp.concatenate([piece[:, :128], piece[:, 128:]], axis=0))
            z = mm(rf[...], jnp.concatenate(parts, axis=1))
            z_re, z_im = z[:half], z[half:]
            gain = lax.rsqrt(lax.rsqrt(z_re * z_re + z_im * z_im + 1.0))
            q = jnp.concatenate([(z_re * gain).astype(BF), (z_im * gain).astype(BF)], axis=0)
            u = mm(ri[...], q).astype(BF)
            parts = []
            for n in range(len(members)):
                at = slice(128 * n, 128 * n + 128)
                parts.append(jnp.concatenate([u[:rows, at], u[rows:, at]], axis=1))
            v = mm(jnp.concatenate(parts, axis=0), ci[...]) * tp[...]
            for n, t in enumerate(members):
                piece = v[n * rows : (n + 1) * rows]
                if t < even_tiles:
                    at = slice(128 * t, 128 * t + 128)
                    even_re[:, at] = piece[:, :128]
                    even_im[:, at] = piece[:, 128:]
                else:
                    at = slice(128 * (t - even_tiles), 128 * (t - even_tiles) + 128)
                    odd_re[:, at] = piece[:, :128]
                    odd_im[:, at] = piece[:, 128:]
        f_re = even_re[...] + odd_re[:, HALF : HALF + cols]
        f_im = even_im[...] + odd_im[:, HALF : HALF + cols]
        out[i] = (f_im * lax.rsqrt(f_re * f_re + f_im * f_im + 1.0)).astype(BF)
        return carry

    lax.fori_loop(0, group, one, 0)


def filtered_sines(re, im, halos, tables):
    count, rows, cols = re.shape
    group = 8 if count % 8 == 0 else count
    wide = -(-(cols + PATCH) // 128) * 128
    extended = rows + PATCH
    whole = pl.BlockSpec((group, rows, cols), lambda i: (i, 0, 0))
    part = pl.BlockSpec((group, HALF, cols), lambda i: (i, 0, 0))
    fixed = [pl.BlockSpec(t.shape, lambda i: (0, 0)) for t in tables]
    flops = 2 * count * 9 * (extended + 5 * rows) * 65536
    return pl.pallas_call(
        filter_kernel,
        grid=(count // group,),
        in_specs=[whole, whole, part, part, part, part] + fixed,
        out_specs=whole,
        out_shape=jax.ShapeDtypeStruct((count, rows, cols), BF),
        scratch_shapes=[
            pltpu.VMEM((extended, wide), BF),
            pltpu.VMEM((extended, wide), BF),
            pltpu.VMEM((rows, cols), F32),
            pltpu.VMEM((rows, cols), F32),
            pltpu.VMEM((rows, wide), F32),
            pltpu.VMEM((rows, wide), F32),
        ],
        compiler_params=pltpu.CompilerParams(vmem_limit_bytes=40 << 20),
        cost_estimate=pl.CostEstimate(
            flops=flops, bytes_accessed=count * rows * cols * 8, transcendentals=0
        ),
        name="goldstein",
    )(re, im, *halos, *tables)


def inverse_kernel(steps, pairs, pairs_t, k_hi, k_lo, p_hi, p_lo):
    n = pairs.shape[0]
    dates = p_hi.shape[0]
    a, b = pairs[:, 0:1], pairs[:, 1:2]
    at, bt = pairs_t[0:1, :], pairs_t[1:2, :]
    one = lambda m: jnp.where(m, 1.0, 0.0)
    row = lax.broadcasted_iota(jnp.int32, (n, n), 0)
    col = lax.broadcasted_iota(jnp.int32, (n, n), 1)
    eye = one(row == col)
    matrix = one(a == at) + one(b == bt) - one(a == bt) - one(b == at) + eye
    exact = matrix.astype(BF)
    top = jnp.max(jnp.sum(jnp.abs(matrix), axis=1, keepdims=True), axis=0, keepdims=True)
    rho = (top - 1.0) / (top + 1.0)
    x = eye * (2.0 / (top + 1.0))

    def refine(_, carry):
        x, rho = carry
        xh, xm, xl = split3(x)
        residual = eye - (mm(exact, xh) + (mm(exact, xm) + mm(exact, xl)))
        scale = 2.0 / (2.0 - rho * rho)
        return (x + mm3(x, residual)) * scale, rho * rho / (2.0 - rho * rho)

    x, rho = lax.fori_loop(0, steps, refine, (x, rho))
    xh, xm, xl = split3(x)
    date = lax.broadcasted_iota(jnp.int32, (dates, n), 0)
    design_t = (one(date == bt) - one(date == at)).astype(BF)
    k_hi[...], k_lo[...] = split2(x)
    p_hi[...], p_lo[...] = split2(mm(design_t, xh) + (mm(design_t, xm) + mm(design_t, xl)))


def inverse_tables(date_pairs):
    n = date_pairs.shape[0]
    top, steps = 2.0 * n + 1.0, 0
    rho = (top - 1.0) / (top + 1.0)
    while rho > 1e-7:
        rho = rho * rho / (2.0 - rho * rho)
        steps += 1
    vmem = pl.BlockSpec(memory_space=pltpu.VMEM)
    return pl.pallas_call(
        functools.partial(inverse_kernel, steps),
        in_specs=[vmem, vmem],
        out_specs=[vmem] * 4,
        out_shape=[jax.ShapeDtypeStruct((n, n), BF)] * 2
        + [jax.ShapeDtypeStruct((NDATES, n), BF)] * 2,
        compiler_params=pltpu.CompilerParams(vmem_limit_bytes=40 << 20),
        cost_estimate=pl.CostEstimate(
            flops=steps * 6 * 4 * n**3, bytes_accessed=8 * n * n, transcendentals=0
        ),
        name="newton",
    )(date_pairs, date_pairs.T)


def invert_kernel(d_ref, k_hi, k_lo, p_hi, p_lo, out):
    d = d_ref[0].astype(F32)
    clip = lambda r: jnp.minimum(jnp.maximum(r, -huber_threshold), huber_threshold)

    def apply(high, low, v):
        vh, vl = split2(v)
        return mm(high[...], vh) + (mm(low[...], vh) + mm(high[...], vl))

    total = clip(d)
    for _ in range(ITERS - 1):
        total = total + clip(d - total + apply(k_hi, k_lo, total))
    out[0] = apply(p_hi, p_lo, total).astype(out.dtype)


def invert(sines, tables):
    strips, n, cols = sines.shape
    fixed = [pl.BlockSpec(t.shape, lambda i: (0, 0)) for t in tables]
    return pl.pallas_call(
        invert_kernel,
        grid=(strips,),
        in_specs=[pl.BlockSpec((1, n, cols), lambda i: (i, 0, 0))] + fixed,
        out_specs=pl.BlockSpec((1, NDATES, cols), lambda i: (i, 0, 0)),
        out_shape=jax.ShapeDtypeStruct((strips, NDATES, cols), BF),
        compiler_params=pltpu.CompilerParams(vmem_limit_bytes=40 << 20),
        name="huber",
    )(sines, *tables)


def gauss_matrix(size_out, size_in, offset):
    distance = np.arange(size_in)[None, :] - offset - np.arange(size_out)[:, None]
    kernel = np.exp(-0.5 * (distance.astype(np.float32) / np.float32(blur_sigma)) ** 2)
    return np.where(np.abs(distance) <= RADIUS, kernel, 0.0).astype(np.float32)


def blur_kernel(own, low, high, rk, ck_hi, ck_lo, inv_row, inv_col, corrected, atmosphere):
    group, rows, cols = own.shape
    pieces = []
    for i in range(group):
        extended = jnp.concatenate([low[i], own[i], high[i]], axis=0)
        both = mm(rk[...], extended)
        pieces.append((both[:rows] + both[rows:]).astype(BF))
    stacked = jnp.concatenate(pieces, axis=0)
    smooth = mm(stacked, ck_hi[...]) + mm(stacked, ck_lo[...])
    for i in range(group):
        air = smooth[i * rows : (i + 1) * rows] * inv_row[...] * inv_col[...]
        atmosphere[i] = air
        corrected[i] = own[i].astype(F32) - air


def blur(own, low, high):
    dates, rows, cols = own.shape
    group = next(g for g in (8, 5, 4, 2, 1) if dates % g == 0)
    hi = lambda v: v.astype(BF)
    lo = lambda v: (v - v.astype(BF).astype(np.float32)).astype(BF)
    row_filter = gauss_matrix(rows, rows + 2 * RADIUS, RADIUS)
    col_filter = gauss_matrix(cols, cols, 0)
    row_tables = jnp.asarray(np.concatenate([hi(row_filter), lo(row_filter)], axis=0))
    source = lax.axis_index("row") * rows - RADIUS + jnp.arange(rows + 2 * RADIUS, dtype=jnp.int32)
    inside = (source >= 0) & (source < rows * lax.axis_size("row"))
    row_weight = jnp.sum(jnp.where(inside[None, :], jnp.asarray(row_filter), 0.0), axis=1)
    fixed = [
        row_tables,
        jnp.asarray(hi(col_filter)),
        jnp.asarray(lo(col_filter)),
        (1.0 / row_weight)[:, None],
        jnp.asarray(1.0 / col_filter.sum(axis=0, dtype=np.float32))[None, :],
    ]
    block = pl.BlockSpec((group, rows, cols), lambda i: (i, 0, 0))
    edge = pl.BlockSpec((group, RADIUS, cols), lambda i: (i, 0, 0))
    return pl.pallas_call(
        blur_kernel,
        grid=(dates // group,),
        in_specs=[block, edge, edge] + [pl.BlockSpec(t.shape, lambda i: (0, 0)) for t in fixed],
        out_specs=[block, block],
        out_shape=[jax.ShapeDtypeStruct((dates, rows, cols), F32)] * 2,
        compiler_params=pltpu.CompilerParams(vmem_limit_bytes=50 << 20),
        name="blur",
    )(own, low, high, *fixed)


def from_neighbours(block, axis, dim, width):
    count = lax.axis_size(axis)
    forward = [(i, i + 1) for i in range(count - 1)]
    backward = [(target, source) for source, target in forward]
    low = lax.ppermute(
        lax.slice_in_dim(block, block.shape[dim] - width, None, axis=dim), axis, forward
    )
    high = lax.ppermute(lax.slice_in_dim(block, 0, width, axis=dim), axis, backward)
    return low, high


def on_device(ifg_real, ifg_imag, date_pairs):
    count, rows, cols = ifg_real.shape
    parts = lax.axis_size("ifg")
    chunks = CHUNKS if count % (8 * CHUNKS) == 0 else 1
    size = count // chunks
    strip = rows // parts
    tables = spectral_tables(rows)
    halos = []
    for n in range(chunks):
        at = slice(n * size, (n + 1) * size)
        low_re, high_re = from_neighbours(ifg_real[at], "row", 1, HALF)
        low_im, high_im = from_neighbours(ifg_imag[at], "row", 1, HALF)
        halos.append((low_re, low_im, high_re, high_im))
    solver = inverse_tables(date_pairs)
    arrived = []
    for n in range(chunks):
        at = slice(n * size, (n + 1) * size)
        sines = filtered_sines(ifg_real[at], ifg_imag[at], halos[n], tables)
        sines = sines.reshape(size, parts, strip, cols).transpose(1, 2, 0, 3)
        arrived.append(lax.all_to_all(sines, "ifg", split_axis=0, concat_axis=0, tiled=True))
    sines = jnp.stack(arrived)
    sines = sines.transpose(2, 1, 0, 3, 4).reshape(strip, parts * count, cols)
    series = invert(sines, solver)
    mine = NDATES // parts
    series = series.reshape(strip, parts, mine, cols).transpose(1, 2, 0, 3)
    values = lax.all_to_all(series, "ifg", split_axis=0, concat_axis=0, tiled=True)
    values = values.transpose(1, 0, 2, 3).reshape(mine, rows, cols)
    low, high = from_neighbours(values, "row", 1, RADIUS)
    return tuple(blur(values, low, high))


def solution(mesh):
    placed = (P("ifg", "row", None), P("ifg", "row", None), P())
    return jax.shard_map(
        on_device,
        mesh=mesh,
        in_specs=placed,
        out_specs=(P("ifg", "row", None), P("ifg", "row", None)),
        check_vma=False,
    )
```

time: 1270 us -> 237 us (0.19)
  local copies, waits for them, and re-layouts: 552 us -> 12.7 us
  other arithmetic: 282 us -> 1.53 us
  matrix products: 275 us -> 0 us
  Pallas kernels: 0 us -> 118 us
  blocking collectives: 64.8 us -> 34.6 us
  waiting for transfers between devices: 51.7 us -> 29.4 us
  starting transfers between devices: 18.5 us -> 38.6 us
    dot_general x360 -> x0, matrix products: 266 us -> none  [the longest x64 71.1 us: filter_block(): jnp.einsum('anbcl,lm->anbcm', stacked, forward, preferred_element_type=jn...]
    another operation x139 -> x0, local copies, waits for them, and re-layouts: 161 us -> none  [the longest x128 157 us: filter_block(): pieces = jnp.stack([weighted[..., :PATCH], weighted[..., PATCH:]], axis=1)]
    slice x244 -> x4, local copies, waits for them, and re-layouts: 124 us -> 5.45 us  [the longest x3 5.08 us: from_neighbours(): lax.slice_in_dim(block, 0, width, axis=dim)]
    pallas_call x0 -> x5, Pallas kernels: none -> 118 us  [the longest x2 93.1 us: filtered_sines(): pl.pallas_call(filter_kernel, grid=(count // group,), in_specs=[whole, wh...]
    another operation x36 -> x0, other arithmetic: 97.3 us -> none  [the longest x10 50.9 us: projection(): cholesky_factor = jnp.linalg.cholesky(gram)]
    broadcast_in_dim x17 -> x0, other arithmetic: 63.7 us -> none  [on_device(): lax.map(run_block, block_list)]
    while x192 -> x0, local copies, waits for them, and re-layouts: 44.4 us -> none
    unnamed x38 -> x33, local copies, waits for them, and re-layouts: 45.6 us -> 2.01 us
  transfers between devices with their start and end apart: 5 -> 12, of which waited for: 3 -> 5; matrix products, arithmetic and copies ran while one was open for 9% -> 2% of each run, Pallas kernels for 0% -> 42%
where the time goes in v1:
time: 237 us; the launch traced here: 236 us
  Pallas kernels  118 us (50%)
  starting transfers between devices  38.6 us (16%)
  blocking collectives  34.6 us (15%)
  waiting for transfers between devices  29.4 us (12%)
  local copies, waits for them, and re-layouts  12.7 us (5%)
    pallas_call x2, Pallas kernels, filtered_sines(): pl.pallas_call(filter_kernel, grid=(count // group,), in_specs=[whole, wh...  93.1 us
    all_to_all x1, blocking collectives, on_device(): lax.all_to_all(series, 'ifg', split_axis=0, concat_axis=0, tiled=True)  34.6 us
    ppermute x5, starting transfers between devices, from_neighbours(): lax.ppermute(lax.slice_in_dim(block, block.shape[dim] - width, None, axis...  23.4 us
    ppermute x5, waiting for transfers between devices, from_neighbours(): lax.ppermute(lax.slice_in_dim(block, 0, width, axis=dim), axis, backward)  19.6 us
    pallas_call x1, Pallas kernels, invert(): pl.pallas_call(invert_kernel, grid=(strips,), in_specs=[pl.BlockSpec((1,...  10.3 us
    all_to_all x2, waiting for transfers between devices, on_device(): lax.all_to_all(sines, 'ifg', split_axis=0, concat_axis=0, tiled=True)  8.79 us
    all_to_all x2, starting transfers between devices, on_device(): lax.all_to_all(sines, 'ifg', split_axis=0, concat_axis=0, tiled=True)  8.34 us
    pallas_call x1, Pallas kernels, blur(): pl.pallas_call(blur_kernel, grid=(dates // group,), in_specs=[block, edge...  8.18 us
  transfers between devices with their start and end apart: 12, of which 5 were waited for; matrix products, arithmetic and copies ran while one was open for 2% of the time, Pallas kernels for 42%

profile of v1, /device:TPU:0, one launch (start us, length us, event | category | flops | bytes accessed | tf_op | source)
XLA Modules:
  0.0 235.9 jit_solution(7112358730877991462)
XLA Ops:
  0.6 0.0 copy-start.13
  0.6 2.9 %fusion.2 = (bf16[16,32,512]{2,1,0:T(8,128)(2,1)}, bf16[16,32,512]{2,1,0:T(8,128)(2,1)}, bf16[16,32,512]{2,1,0:T(8,128)(2,1)S(1)}, bf16[16,32,512]{2,1,0:T(8,128)(2,1)S(1)}) fusion(bf16[32,64,512]{2,1,0:T(8,128)(2,1)} %param.13), kind=kLoop, calls=%fused_computation.10 | loop fusion | bytes 4194304 | tf_op jit(solution)/shard_map/slice | solution.py:327
  3.5 1.4 collective-permute-start.6
  5.0 5.6 %collective-permute-start.4 = (bf16[16,32,512]{2,1,0:T(8,128)(2,1)S(1)}, bf16[16,32,512]{2,1,0:T(8,128)(2,1)S(1)}, u32[]{:S(2)}, u32[]{:S(2)}) collective-permute-start(bf16[16,32,512]{2,1,0:T(8,128)(2,1)S(1)} %get-tuple-element.19), channel_id=1, source_target_pairs={{0,1},{1,2},{2,3},{4,5},{5,6},{6,7},{8,9},{9,10},{10,11},{12,13},{... | collective-permute-start | bytes 1572872 | tf_op jit(solution)/shard_map/ppermute | solution.py:324
  10.6 0.0 copy-done.13
  10.6 1.2 fusion.1
  11.8 1.3 collective-permute-start.7
  13.1 4.6 %collective-permute-start.5 = (bf16[16,32,512]{2,1,0:T(8,128)(2,1)S(1)}, bf16[16,32,512]{2,1,0:T(8,128)(2,1)S(1)}, u32[]{:S(2)}, u32[]{:S(2)}) collective-permute-start(bf16[16,32,512]{2,1,0:T(8,128)(2,1)S(1)} %get-tuple-element.15), channel_id=1, source_target_pairs={{0,1},{1,2},{2,3},{4,5},{5,6},{6,7},{8,9},{9,10},{10,11},{12,13},{... | collective-permute-start | bytes 1572872 | tf_op jit(solution)/shard_map/ppermute | solution.py:324
  17.7 0.0 copy-start.5
  17.7 0.0 copy-start.6
  17.8 0.0 copy-start.7
  17.8 0.0 copy-start.9
  17.8 0.0 copy-start.11
  17.8 1.4 collective-permute-start.2
  19.2 0.0 copy-done.14
  19.2 0.4 fusion.3
  19.6 1.8 collective-permute-done.6.high_re
  21.4 3.9 %collective-permute-start = (bf16[16,32,512]{2,1,0:T(8,128)(2,1)}, bf16[16,32,512]{2,1,0:T(8,128)(2,1)S(1)}, u32[]{:S(2)}, u32[]{:S(2)}) collective-permute-start(bf16[16,32,512]{2,1,0:T(8,128)(2,1)} %get-tuple-element.17), channel_id=1, source_target_pairs={{0,1},{1,2},{2,3},{4,5},{5,6},{6,7},{8,9},{9,10},{10,11},{12,13},{... | collective-permute-start | bytes 1572872 | tf_op jit(solution)/shard_map/ppermute | solution.py:324
  25.3 0.0 collective-permute-done.4.low_re
  25.3 1.3 collective-permute-start.3
  26.6 6.0 %collective-permute-done.7.high_im = bf16[16,32,512]{2,1,0:T(8,128)(2,1)S(1)} collective-permute-done((bf16[16,32,512]{2,1,0:T(8,128)(2,1)S(1)}, bf16[16,32,512]{2,1,0:T(8,128)(2,1)S(1)}, u32[]{:S(2)}, u32[]{:S(2)}) %collective-permute-start.7) | collective-permute-done | bytes 524320 | tf_op jit(solution)/shard_map/ppermute | solution.py:327
  32.6 4.7 %collective-permute-start.1 = (bf16[16,32,512]{2,1,0:T(8,128)(2,1)}, bf16[16,32,512]{2,1,0:T(8,128)(2,1)}, u32[]{:S(2)}, u32[]{:S(2)}) collective-permute-start(bf16[16,32,512]{2,1,0:T(8,128)(2,1)} %get-tuple-element.13), channel_id=1, source_target_pairs={{0,1},{1,2},{2,3},{4,5},{5,6},{6,7},{8,9},{9,10},{10,11},{12,13},{... | collective-permute-start | bytes 1572872 | tf_op jit(solution)/shard_map/ppermute | solution.py:324
  37.3 0.0 collective-permute-done.5.low_im
  37.3 0.0 copy-done.5
  37.3 0.0 copy-done.6
  37.4 46.0 %goldstein.3 = bf16[16,64,512]{2,1,0:T(8,128)(2,1)S(1)} custom-call(bf16[16,64,512]{2,1,0:T(8,128)(2,1)S(1)} %get-tuple-element.24.re, bf16[16,64,512]{2,1,0:T(8,128)(2,1)S(1)} %get-tuple-element.21.im, bf16[16,32,512]{2,1,0:T(8,128)(2,1)S(1)} %collective-permute-done.4.low_re, bf16[16,32,512]{2,1,0:T(8,128)(2,1)S(1)} %collective-permute-done.5.low_im, ...), custom_call_target="tpu_custom_call" | custom-call | flops 8455716864 | bytes 4194304 | tf_op jit(solution)/shard_map/goldstein/pallas_call | solution.py:166
  83.4 1.5 copy.39
  84.9 4.2 %all-to-all-start.1 = ((bf16[8,8,16,512]{3,2,1,0:T(8,128)(2,1)}), bf16[8,8,16,512]{3,2,1,0:T(8,128)(2,1)}, u32[]{:S(2)}, u32[]{:S(2)}) async-start(bf16[8,8,16,512]{3,2,1,0:T(8,128)(2,1)} %bitcast.31), calls=%async_computation.1 | async-start | bytes 2097152 | tf_op jit(solution)/shard_map/all_to_all | solution.py:350
  89.2 0.0 collective-permute-done.2.high_re
  89.2 0.0 collective-permute-done.low_re
  89.2 0.0 collective-permute-done.3.high_im
  89.2 0.0 collective-permute-done.1.low_im
  89.2 0.0 copy-start.8
  89.3 0.9 copy-done.8
  90.2 0.9 copy-done.10
  91.0 47.1 %goldstein.2 = bf16[16,64,512]{2,1,0:T(8,128)(2,1)S(1)} custom-call(bf16[16,64,512]{2,1,0:T(8,128)(2,1)S(1)} %get-tuple-element.25.re, bf16[16,64,512]{2,1,0:T(8,128)(2,1)S(1)} %get-tuple-element.20.im, bf16[16,32,512]{2,1,0:T(8,128)(2,1)S(1)} %collective-permute-done.low_re, bf16[16,32,512]{2,1,0:T(8,128)(2,1)} %collective-permute-done.1.low_im, ...), custom_call_target="tpu_custom_call" | custom-call | flops 8455716864 | bytes 4194304 | tf_op jit(solution)/shard_map/goldstein/pallas_call | solution.py:166
  138.1 0.0 copy-start.3
  138.1 1.5 copy.40
  139.7 0.0 all-to-all-done.1
  139.7 4.1 %all-to-all-start = ((bf16[8,8,16,512]{3,2,1,0:T(8,128)(2,1)}), bf16[8,8,16,512]{3,2,1,0:T(8,128)(2,1)S(1)}, u32[]{:S(2)}, u32[]{:S(2)}) async-start(bf16[8,8,16,512]{3,2,1,0:T(8,128)(2,1)} %bitcast.24), calls=%async_computation | async-start | bytes 2097152 | tf_op jit(solution)/shard_map/all_to_all | solution.py:350
  143.8 0.1 copy.30.pairs
  143.9 6.4 %newton.1 = (bf16[256,256]{1,0:T(8,128)(2,1)S(1)}, bf16[256,256]{1,0:T(8,128)(2,1)S(1)}, bf16[320,256]{1,0:T(8,128)(2,1)S(1)}, bf16[320,256]{1,0:T(8,128)(2,1)S(1)}) custom-call(s32[256,2]{1,0:T(8,128)S(1)} %copy.30.pairs, s32[2,256]{1,0:T(2,128)S(1)} %bitcast.29), custom_call_target="tpu_custom_call" | custom-call | flops 3221225472 | bytes 524288 | tf_op jit(solution)/shard_map/newton/pallas_call | solution.py:226
  150.3 8.8 %all-to-all-done = bf16[8,8,16,512]{3,2,1,0:T(8,128)(2,1)S(1)} async-done(((bf16[8,8,16,512]{3,2,1,0:T(8,128)(2,1)}), bf16[8,8,16,512]{3,2,1,0:T(8,128)(2,1)S(1)}, u32[]{:S(2)}, u32[]{:S(2)}) %all-to-all-start) | async-done | bytes 1048608 | tf_op jit(solution)/shard_map/all_to_all | solution.py:350
  159.1 1.4 maximum_bitcast_fusion
  160.6 0.2 copy.29
  160.8 10.3 %huber.1 = bf16[8,320,512]{2,1,0:T(8,128)(2,1)S(1)} custom-call(bf16[8,256,512]{2,1,0:T(8,128)(2,1)S(1)} %bitcast.26, bf16[256,256]{1,0:T(8,128)(2,1)S(1)} %get-tuple-element.6.k_hi, bf16[256,256]{1,0:T(8,128)(2,1)S(1)} %get-tuple-element.7.k_lo, bf16[320,256]{1,0:T(8,128)(2,1)S(1)} %get-tuple-element.8.p_hi, bf16[320,256]{1,0:T(8,128)(2,1)S(1)} %get-tuple-element.9.p_lo), custom_call_target="tpu_custom_call" | custom-call | tf_op jit(solution)/shard_map/huber/pallas_call | solution.py:257
  171.2 1.5 copy.38
  172.6 34.6 %all_to_all.15 = bf16[8,40,8,512]{3,2,1,0:T(8,128)(2,1)S(1)} all-to-all(bf16[8,40,8,512]{3,2,1,0:T(8,128)(2,1)S(1)} %bitcast.30), channel_id=1, replica_groups=mesh['ifg'=8,'row'=4] {'ifg'}, dimensions={0} | all-to-all | bytes 5242880 | tf_op jit(solution)/shard_map/all_to_all | solution.py:356
  207.3 0.3 copy_bitcast_fusion.own
  207.6 0.0 copy-start.15
  207.6 0.0 copy-start
  207.7 0.0 copy-start.1
  207.7 0.0 copy-start.2
  207.7 0.0 copy-start.4
  207.7 0.9 fusion
  208.6 1.4 collective-permute-start.9
  210.1 4.6 %collective-permute-start.8 = (bf16[40,16,512]{2,1,0:T(8,128)(2,1)S(1)}, bf16[40,16,512]{2,1,0:T(8,128)(2,1)S(1)}, u32[]{:S(2)}, u32[]{:S(2)}) collective-permute-start(bf16[40,16,512]{2,1,0:T(8,128)(2,1)S(1)} %get-tuple-element.11), channel_id=1, source_target_pairs={{0,1},{1,2},{2,3},{4,5},{5,6},{6,7},{8,9},{9,10},{10,11},{12,13},{... | collective-permute-start | bytes 1966088 | tf_op jit(solution)/shard_map/ppermute | solution.py:324
  214.7 0.0 copy-done.15
  214.7 0.1 select_reduce_fusion
  214.8 0.1 copy.33.inv_row
  214.9 11.9 %collective-permute-done.9.high = bf16[40,16,512]{2,1,0:T(8,128)(2,1)S(1)} collective-permute-done((bf16[40,16,512]{2,1,0:T(8,128)(2,1)}, bf16[40,16,512]{2,1,0:T(8,128)(2,1)S(1)}, u32[]{:S(2)}, u32[]{:S(2)}) %collective-permute-start.9) | collective-permute-done | bytes 655392 | tf_op jit(solution)/shard_map/ppermute | solution.py:327
  226.8 1.0 collective-permute-done.8.low
  227.8 0.0 copy-done.4
  227.8 8.2 %blur.1 = (f32[40,64,512]{2,1,0:T(8,128)}, f32[40,64,512]{2,1,0:T(8,128)}) custom-call(bf16[40,64,512]{2,1,0:T(8,128)(2,1)} %copy-done.12, bf16[40,16,512]{2,1,0:T(8,128)(2,1)S(1)} %collective-permute-done.8.low, bf16[40,16,512]{2,1,0:T(8,128)(2,1)S(1)} %collective-permute-done.9.high, bf16[128,96]{1,0:T(8,128)(2,1)S(1)} %copy-done.2, ...), custom_call_target="tpu_custom_call" | custom-call | tf_op jit(solution)/shard_map/blur/pallas_call | solution.py:309
  (13 shorter events, 0.0 us)
Async XLA Ops:
  0.6 10.0 %copy-start.13 = (bf16[32,64,512]{2,1,0:T(8,128)(2,1)S(1)}, bf16[32,64,512]{2,1,0:T(8,128)(2,1)}, u32[]{:S(2)}) copy-start(bf16[32,64,512]{2,1,0:T(8,128)(2,1)} %param.14) | copy-start | bytes 6291460
  3.5 15.7 %copy-start.14 = (bf16[32,64,512]{2,1,0:T(8,128)(2,1)S(1)}, bf16[32,64,512]{2,1,0:T(8,128)(2,1)}, u32[]{:S(2)}) copy-start(bf16[32,64,512]{2,1,0:T(8,128)(2,1)} %param.13) | copy-start | bytes 6291460
  3.5 17.8 %collective-permute-start.6 = (bf16[16,32,512]{2,1,0:T(8,128)(2,1)S(1)}, bf16[16,32,512]{2,1,0:T(8,128)(2,1)S(1)}, u32[]{:S(2)}, u32[]{:S(2)}) collective-permute-start(bf16[16,32,512]{2,1,0:T(8,128)(2,1)S(1)} %get-tuple-element.18), channel_id=1, source_target_pairs={{1,0},{2,1},{3,2},{5,4},{6,5},{7,6},{9,8},{10,9},{11,10},{13,12},{... | collective-permute-start | bytes 1572872 | tf_op jit(solution)/shard_map/ppermute | solution.py:327
  5.0 20.4 %collective-permute-start.4 = (bf16[16,32,512]{2,1,0:T(8,128)(2,1)S(1)}, bf16[16,32,512]{2,1,0:T(8,128)(2,1)S(1)}, u32[]{:S(2)}, u32[]{:S(2)}) collective-permute-start(bf16[16,32,512]{2,1,0:T(8,128)(2,1)S(1)} %get-tuple-element.19), channel_id=1, source_target_pairs={{0,1},{1,2},{2,3},{4,5},{5,6},{6,7},{8,9},{9,10},{10,11},{12,13},{... | collective-permute-start | bytes 1572872 | tf_op jit(solution)/shard_map/ppermute | solution.py:324
  11.8 20.8 %collective-permute-start.7 = (bf16[16,32,512]{2,1,0:T(8,128)(2,1)S(1)}, bf16[16,32,512]{2,1,0:T(8,128)(2,1)S(1)}, u32[]{:S(2)}, u32[]{:S(2)}) collective-permute-start(bf16[16,32,512]{2,1,0:T(8,128)(2,1)S(1)} %get-tuple-element.14), channel_id=1, source_target_pairs={{1,0},{2,1},{3,2},{5,4},{6,5},{7,6},{9,8},{10,9},{11,10},{13,12},{... | collective-permute-start | bytes 1572872 | tf_op jit(solution)/shard_map/ppermute | solution.py:327
  13.1 24.2 %collective-permute-start.5 = (bf16[16,32,512]{2,1,0:T(8,128)(2,1)S(1)}, bf16[16,32,512]{2,1,0:T(8,128)(2,1)S(1)}, u32[]{:S(2)}, u32[]{:S(2)}) collective-permute-start(bf16[16,32,512]{2,1,0:T(8,128)(2,1)S(1)} %get-tuple-element.15), channel_id=1, source_target_pairs={{0,1},{1,2},{2,3},{4,5},{5,6},{6,7},{8,9},{9,10},{10,11},{12,13},{... | collective-permute-start | bytes 1572872 | tf_op jit(solution)/shard_map/ppermute | solution.py:324
  17.7 19.6 %copy-start.5 = (bf16[384,256]{1,0:T(8,128)(2,1)S(1)}, bf16[384,256]{1,0:T(8,128)(2,1)}, u32[]{:S(2)}) copy-start(bf16[384,256]{1,0:T(8,128)(2,1)} %constant.38.clone.rf) | copy-start | bytes 589828
  17.7 19.6 %copy-start.6 = (bf16[256,256]{1,0:T(8,128)(2,1)S(1)}, bf16[256,256]{1,0:T(8,128)(2,1)}, u32[]{:S(2)}) copy-start(bf16[256,256]{1,0:T(8,128)(2,1)} %constant.40.clone.ci) | copy-start | bytes 393220
  17.8 19.6 %copy-start.7 = (bf16[256,256]{1,0:T(8,128)(2,1)S(1)}, bf16[256,256]{1,0:T(8,128)(2,1)}, u32[]{:S(2)}) copy-start(bf16[256,256]{1,0:T(8,128)(2,1)} %constant.37.clone.cf) | copy-start | bytes 393220
  17.8 19.6 %copy-start.9 = (bf16[128,384]{1,0:T(8,128)(2,1)S(1)}, bf16[128,384]{1,0:T(8,128)(2,1)}, u32[]{:S(2)}) copy-start(bf16[128,384]{1,0:T(8,128)(2,1)} %constant.39.clone.ri) | copy-start | bytes 294916
  17.8 19.6 %copy-start.11 = (f32[1,256]{1,0:T(1,128)S(1)}, f32[1,256]{1,0:T(1,128)}, u32[]{:S(2)}) copy-start(f32[1,256]{1,0:T(1,128)} %constant.41.clone.tp) | copy-start | bytes 3076
  17.8 71.4 %collective-permute-start.2 = (bf16[16,32,512]{2,1,0:T(8,128)(2,1)}, bf16[16,32,512]{2,1,0:T(8,128)(2,1)S(1)}, u32[]{:S(2)}, u32[]{:S(2)}) collective-permute-start(bf16[16,32,512]{2,1,0:T(8,128)(2,1)} %get-tuple-element.16), channel_id=1, source_target_pairs={{1,0},{2,1},{3,2},{5,4},{6,5},{7,6},{9,8},{10,9},{11,10},{13,12},{... | collective-permute-start | bytes 1572872 | tf_op jit(solution)/shard_map/ppermute | solution.py:327
  21.4 67.8 %collective-permute-start = (bf16[16,32,512]{2,1,0:T(8,128)(2,1)}, bf16[16,32,512]{2,1,0:T(8,128)(2,1)S(1)}, u32[]{:S(2)}, u32[]{:S(2)}) collective-permute-start(bf16[16,32,512]{2,1,0:T(8,128)(2,1)} %get-tuple-element.17), channel_id=1, source_target_pairs={{0,1},{1,2},{2,3},{4,5},{5,6},{6,7},{8,9},{9,10},{10,11},{12,13},{... | collective-permute-start | bytes 1572872 | tf_op jit(solution)/shard_map/ppermute | solution.py:324
  25.3 63.9 %collective-permute-start.3 = (bf16[16,32,512]{2,1,0:T(8,128)(2,1)}, bf16[16,32,512]{2,1,0:T(8,128)(2,1)}, u32[]{:S(2)}, u32[]{:S(2)}) collective-permute-start(bf16[16,32,512]{2,1,0:T(8,128)(2,1)} %get-tuple-element.12), channel_id=1, source_target_pairs={{1,0},{2,1},{3,2},{5,4},{6,5},{7,6},{9,8},{10,9},{11,10},{13,12},{... | collective-permute-start | bytes 1572872 | tf_op jit(solution)/shard_map/ppermute | solution.py:327
  32.6 56.6 %collective-permute-start.1 = (bf16[16,32,512]{2,1,0:T(8,128)(2,1)}, bf16[16,32,512]{2,1,0:T(8,128)(2,1)}, u32[]{:S(2)}, u32[]{:S(2)}) collective-permute-start(bf16[16,32,512]{2,1,0:T(8,128)(2,1)} %get-tuple-element.13), channel_id=1, source_target_pairs={{0,1},{1,2},{2,3},{4,5},{5,6},{6,7},{8,9},{9,10},{10,11},{12,13},{... | collective-permute-start | bytes 1572872 | tf_op jit(solution)/shard_map/ppermute | solution.py:324
  84.9 54.7 %all-to-all-start.1 = ((bf16[8,8,16,512]{3,2,1,0:T(8,128)(2,1)}), bf16[8,8,16,512]{3,2,1,0:T(8,128)(2,1)}, u32[]{:S(2)}, u32[]{:S(2)}) async-start(bf16[8,8,16,512]{3,2,1,0:T(8,128)(2,1)} %bitcast.31), calls=%async_computation.1 | async-start | bytes 2097152 | tf_op jit(solution)/shard_map/all_to_all | solution.py:350
  89.2 0.9 copy-start.8
  90.2 0.9 copy-start.10
  138.1 5.7 %copy-start.3 = (s32[256,2]{0,1:T(2,128)S(1)}, s32[256,2]{0,1:T(2,128)}, u32[]{:S(2)}) copy-start(s32[256,2]{0,1:T(2,128)} %param.15) | copy-start | bytes 6148
  139.7 19.5 %all-to-all-start = ((bf16[8,8,16,512]{3,2,1,0:T(8,128)(2,1)}), bf16[8,8,16,512]{3,2,1,0:T(8,128)(2,1)S(1)}, u32[]{:S(2)}, u32[]{:S(2)}) async-start(bf16[8,8,16,512]{3,2,1,0:T(8,128)(2,1)} %bitcast.24), calls=%async_computation | async-start | bytes 2097152 | tf_op jit(solution)/shard_map/all_to_all | solution.py:350
  207.6 2.4 %copy-start.12 = (bf16[40,64,512]{2,1,0:T(8,128)(2,1)}, bf16[40,64,512]{2,1,0:T(8,128)(2,1)S(1)}, u32[]{:S(2)}) copy-start(bf16[40,64,512]{2,1,0:T(8,128)(2,1)S(1)} %copy_bitcast_fusion.own) | copy-start | bytes 7864324
  207.6 7.0 %copy-start.15 = (f32[64,96]{1,0:T(8,128)S(1)}, f32[64,96]{1,0:T(8,128)}, u32[]{:S(2)}) copy-start(f32[64,96]{1,0:T(8,128)} %constant.43.clone) | copy-start | bytes 73732
  207.6 20.1 %copy-start = (bf16[512,512]{1,0:T(8,128)(2,1)S(1)}, bf16[512,512]{1,0:T(8,128)(2,1)}, u32[]{:S(2)}) copy-start(bf16[512,512]{1,0:T(8,128)(2,1)} %constant.45.clone.ck_lo) | copy-start | bytes 1572868
  207.7 20.1 %copy-start.1 = (bf16[512,512]{1,0:T(8,128)(2,1)S(1)}, bf16[512,512]{1,0:T(8,128)(2,1)}, u32[]{:S(2)}) copy-start(bf16[512,512]{1,0:T(8,128)(2,1)} %constant.44.clone.ck_hi) | copy-start | bytes 1572868
  207.7 20.1 %copy-start.2 = (bf16[128,96]{1,0:T(8,128)(2,1)S(1)}, bf16[128,96]{1,0:T(8,128)(2,1)}, u32[]{:S(2)}) copy-start(bf16[128,96]{1,0:T(8,128)(2,1)} %constant.42.clone.rk) | copy-start | bytes 73732
  207.7 20.1 %copy-start.4 = (f32[1,512]{1,0:T(1,128)S(1)}, f32[1,512]{1,0:T(1,128)}, u32[]{:S(2)}) copy-start(f32[1,512]{1,0:T(1,128)} %constant.47.inv_col) | copy-start | bytes 6148
  208.6 18.1 %collective-permute-start.9 = (bf16[40,16,512]{2,1,0:T(8,128)(2,1)}, bf16[40,16,512]{2,1,0:T(8,128)(2,1)S(1)}, u32[]{:S(2)}, u32[]{:S(2)}) collective-permute-start(bf16[40,16,512]{2,1,0:T(8,128)(2,1)} %get-tuple-element.10), channel_id=1, source_target_pairs={{1,0},{2,1},{3,2},{5,4},{6,5},{7,6},{9,8},{10,9},{11,10},{13,12},{... | collective-permute-start | bytes 1966088 | tf_op jit(solution)/shard_map/ppermute | solution.py:327
  210.1 17.7 %collective-permute-start.8 = (bf16[40,16,512]{2,1,0:T(8,128)(2,1)S(1)}, bf16[40,16,512]{2,1,0:T(8,128)(2,1)S(1)}, u32[]{:S(2)}, u32[]{:S(2)}) collective-permute-start(bf16[40,16,512]{2,1,0:T(8,128)(2,1)S(1)} %get-tuple-element.11), channel_id=1, source_target_pairs={{0,1},{1,2},{2,3},{4,5},{5,6},{6,7},{8,9},{9,10},{10,11},{12,13},{... | collective-permute-start | bytes 1966088 | tf_op jit(solution)/shard_map/ppermute | solution.py:324

commit v2 on v1

v2 whole, which is shorter than its diff:
```python
import functools
import math

import jax
import jax.numpy as jnp
import numpy as np
from jax import lax
from jax.experimental import pallas as pl
from jax.experimental.pallas import tpu as pltpu
from jax.sharding import PartitionSpec as P

PATCH = 64
HALF = PATCH // 2
RADIUS = 16
NDATES = 320
ITERS = 3

huber_threshold = 0.3
blur_sigma = 5.0

BF = jnp.bfloat16
F32 = jnp.float32


def mm(a, b):
    return jnp.dot(a, b, preferred_element_type=F32)


def split2(x):
    high = x.astype(BF)
    return high, (x - high.astype(F32)).astype(BF)


def split3(x):
    high = x.astype(BF)
    rest = x - high.astype(F32)
    mid = rest.astype(BF)
    return high, mid, (rest - mid.astype(F32)).astype(BF)


def mm3(a, b):
    ah, al = split2(a)
    bh, bl = split2(b)
    return mm(ah, bh) + (mm(ah, bl) + mm(al, bh))


def spectral_tables(local_rows):
    k = np.arange(PATCH)
    angles = ((k[:, None] * k[None, :]) % PATCH).astype(np.float32) * np.float32(
        2.0 * math.pi / PATCH
    )
    scaling = np.float32(1.0 / math.sqrt(PATCH))
    rounded = lambda v: np.asarray(v.astype(np.float32)).astype(BF).astype(np.float32)
    c = rounded(np.cos(angles) * scaling)
    s = rounded(np.sin(angles) * scaling)
    taper = (
        np.sin(np.float32(math.pi) * (k.astype(np.float32) + np.float32(0.5)) / PATCH) ** 2
    ).astype(np.float32)
    two = np.eye(2, dtype=np.float32)
    cc, ss = np.kron(two, c), np.kron(two, s)
    col_forward = np.block([[cc, -ss], [ss, cc]])
    col_inverse = np.block([[cc, ss], [-ss, cc]])
    extended = local_rows + PATCH
    starts = list(range(0, extended - PATCH + 1, HALF))
    count = len(starts)
    row_forward = np.zeros((2, count, PATCH, 2, extended), np.float32)
    row_inverse = np.zeros((2, extended, 2, count, PATCH), np.float32)
    for p, at in enumerate(starts):
        where = slice(at, at + PATCH)
        row_forward[0, p, :, 0, where] = c
        row_forward[0, p, :, 1, where] = s
        row_forward[1, p, :, 0, where] = -s
        row_forward[1, p, :, 1, where] = c
        tc, ts = taper[:, None] * c, taper[:, None] * s
        row_inverse[0, where, 0, p, :] = tc
        row_inverse[0, where, 1, p, :] = -ts
        row_inverse[1, where, 0, p, :] = ts
        row_inverse[1, where, 1, p, :] = tc
    row_forward = row_forward.reshape(2 * count * PATCH, 2 * extended)
    row_inverse = row_inverse[:, HALF : HALF + local_rows].reshape(
        2 * local_rows, 2 * count * PATCH
    )
    return (
        jnp.asarray(col_forward.astype(BF)),
        jnp.asarray(row_forward.astype(BF)),
        jnp.asarray(row_inverse.astype(BF)),
        jnp.asarray(col_inverse.astype(BF)),
        jnp.asarray(np.tile(taper, 4)[None, :]),
    )


def pick(sel, first, second, swapped_at, kept_at):
    zero = jnp.zeros_like(first)
    return jnp.where(sel[swapped_at] > 0, first, jnp.where(sel[kept_at] > 0, second, zero))


def filter_kernel(first, width, split, sel, re, im, one, two, *refs):
    if split:
        one_more, two_more, *refs = refs
    cf, rf, ri, ci, tp, out, pad_re, pad_im, even_re, even_im, odd_re, odd_im = refs
    group, rows, cols = re.shape
    extended = rows + PATCH
    window = width + 128
    start = 128 * first
    per = width // 128
    tiles = [(True, t) for t in range(per)] + [(False, t) for t in range(per + 1)]
    half = rf.shape[0] // 2

    @pl.when(pl.program_id(0) == 0)
    def _():
        pad_re[...] = jnp.zeros_like(pad_re)
        pad_im[...] = jnp.zeros_like(pad_im)

    def halo(part, i):
        p, q = one[part, i], two[part, i]
        if split:
            p = jnp.concatenate([p[:, start:], one_more[part, i]], axis=1)
            q = jnp.concatenate([q[:, start:], two_more[part, i]], axis=1)
        return pick(sel, p, q, 0, 1), pick(sel, p, q, 2, 3)

    def load(i, slot):
        made = []
        for part, own, pad in ((0, re, pad_re), (1, im, pad_im)):
            low, high = halo(part, i)
            x = jnp.concatenate([low, own[i, :, start : start + window], high], axis=0)
            pad[slot, :, HALF : HALF + window] = x
            made.append(x)
        return made

    def pair(step, carry):
        images = [load(2 * step + slot, slot) for slot in range(2)]
        members = [(slot, *tile) for tile in tiles for slot in range(2)]
        blocks = [members[n : n + 2] for n in range(0, len(members), 2)]

        def tile_of(slot, even, t):
            at = slice(start + 128 * t, start + 128 * t + 128)
            if even:
                return jnp.concatenate([x[:, at] for x in images[slot]], axis=1)
            return jnp.concatenate([pad_re[slot, :, at], pad_im[slot, :, at]], axis=1)

        def columns(n):
            stacked = jnp.concatenate([tile_of(*m) for m in blocks[n]], axis=0)
            y = mm(stacked, cf[...]).astype(BF)
            return jnp.concatenate(
                [
                    jnp.concatenate([y[:extended, :128], y[:extended, 128:]], axis=0),
                    jnp.concatenate([y[extended:, :128], y[extended:, 128:]], axis=0),
                ],
                axis=1,
            )

        def spectrum(y):
            z = mm(rf[...], y)
            z_re, z_im = z[:half], z[half:]
            gain = lax.rsqrt(lax.rsqrt(z_re * z_re + z_im * z_im + 1.0))
            return jnp.concatenate([(z_re * gain).astype(BF), (z_im * gain).astype(BF)], axis=0)

        def rows_back(q):
            u = mm(ri[...], q).astype(BF)
            return jnp.concatenate(
                [
                    jnp.concatenate([u[:rows, :128], u[rows:, :128]], axis=1),
                    jnp.concatenate([u[:rows, 128:], u[rows:, 128:]], axis=1),
                ],
                axis=0,
            )

        def columns_back(n, u):
            v = mm(u, ci[...]) * tp[...]
            for m, (slot, even, t) in enumerate(blocks[n]):
                piece = v[m * rows : (m + 1) * rows]
                at = slice(128 * t, 128 * t + 128)
                (even_re if even else odd_re)[slot, :, at] = piece[:, :128]
                (even_im if even else odd_im)[slot, :, at] = piece[:, 128:]

        count = len(blocks)
        y, q, u = {}, {}, {}
        for tick in range(count + 3):
            if tick < count:
                y[tick] = columns(tick)
            if 0 <= tick - 1 < count:
                q[tick - 1] = spectrum(y.pop(tick - 1))
            if 0 <= tick - 2 < count:
                u[tick - 2] = rows_back(q.pop(tick - 2))
            if 0 <= tick - 3 < count:
                columns_back(tick - 3, u.pop(tick - 3))
        for slot in range(2):
            f_re = even_re[slot] + odd_re[slot, :, HALF : HALF + width]
            f_im = even_im[slot] + odd_im[slot, :, HALF : HALF + width]
            out[2 * step + slot] = (f_im * lax.rsqrt(f_re * f_re + f_im * f_im + 1.0)).astype(BF)
        return carry

    lax.fori_loop(0, group // 2, pair, 0)


def filtered_sines(re, im, sel, halos, more, tables, at, count, first, width):
    rows, cols = re.shape[1:]
    group = 8
    extended = rows + PATCH
    skip = at // group
    whole = pl.BlockSpec((group, rows, cols), lambda i: (i + skip, 0, 0))
    edge = pl.BlockSpec((2, group, HALF, width + 128), lambda i: (0, i, 0, 0))
    rest = pl.BlockSpec((2, group, HALF, cols - width - 128), lambda i: (0, i + skip, 0, 0))
    fixed = [pl.BlockSpec(t.shape, lambda i: (0, 0)) for t in tables]
    return pl.pallas_call(
        functools.partial(filter_kernel, first, width, bool(more)),
        grid=(count // group,),
        in_specs=[pl.BlockSpec(memory_space=pltpu.SMEM), whole, whole, edge, edge]
        + [rest] * len(more)
        + fixed,
        out_specs=pl.BlockSpec((group, rows, width), lambda i: (i, 0, 0)),
        out_shape=jax.ShapeDtypeStruct((count, rows, width), BF),
        scratch_shapes=[pltpu.VMEM((2, extended, width + 256), BF)] * 2
        + [pltpu.VMEM((2, rows, width), F32)] * 2
        + [pltpu.VMEM((2, rows, width + 128), F32)] * 2,
        compiler_params=pltpu.CompilerParams(vmem_limit_bytes=32 << 20),
        cost_estimate=pl.CostEstimate(
            flops=count * width * 3000000, bytes_accessed=count * rows * cols * 4, transcendentals=0
        ),
        name="goldstein",
    )(sel, re, im, *halos, *more, *tables)


def inverse_kernel(steps, pairs, pairs_t, k_hi, k_lo, p_hi, p_lo):
    n = pairs.shape[0]
    dates = p_hi.shape[0]
    a, b = pairs[:, 0:1], pairs[:, 1:2]
    at, bt = pairs_t[0:1, :], pairs_t[1:2, :]
    one = lambda m: jnp.where(m, 1.0, 0.0)
    row = lax.broadcasted_iota(jnp.int32, (n, n), 0)
    col = lax.broadcasted_iota(jnp.int32, (n, n), 1)
    eye = one(row == col)
    matrix = one(a == at) + one(b == bt) - one(a == bt) - one(b == at) + eye
    exact = matrix.astype(BF)
    top = jnp.max(jnp.sum(jnp.abs(matrix), axis=1, keepdims=True), axis=0, keepdims=True)
    rho = (top - 1.0) / (top + 1.0)
    x = eye * (2.0 / (top + 1.0))

    def refine(_, carry):
        x, rho = carry
        xh, xm, xl = split3(x)
        residual = eye - (mm(exact, xh) + (mm(exact, xm) + mm(exact, xl)))
        scale = 2.0 / (2.0 - rho * rho)
        return (x + mm3(x, residual)) * scale, rho * rho / (2.0 - rho * rho)

    x, rho = lax.fori_loop(0, steps, refine, (x, rho))
    xh, xm, xl = split3(x)
    date = lax.broadcasted_iota(jnp.int32, (dates, n), 0)
    design_t = (one(date == bt) - one(date == at)).astype(BF)
    k_hi[...], k_lo[...] = split2(x)
    p_hi[...], p_lo[...] = split2(mm(design_t, xh) + (mm(design_t, xm) + mm(design_t, xl)))


def inverse_tables(date_pairs):
    n = date_pairs.shape[0]
    top, steps = 2.0 * n + 1.0, 0
    rho = (top - 1.0) / (top + 1.0)
    while rho > 1e-7:
        rho = rho * rho / (2.0 - rho * rho)
        steps += 1
    vmem = pl.BlockSpec(memory_space=pltpu.VMEM)
    return pl.pallas_call(
        functools.partial(inverse_kernel, steps),
        in_specs=[vmem, vmem],
        out_specs=[vmem] * 4,
        out_shape=[jax.ShapeDtypeStruct((n, n), BF)] * 2
        + [jax.ShapeDtypeStruct((NDATES, n), BF)] * 2,
        compiler_params=pltpu.CompilerParams(vmem_limit_bytes=40 << 20),
        cost_estimate=pl.CostEstimate(
            flops=steps * 6 * 4 * n**3, bytes_accessed=8 * n * n, transcendentals=0
        ),
        name="newton",
    )(date_pairs, date_pairs.T)


def invert_kernel(d_ref, k_hi, k_lo, p_hi, p_lo, out):
    parts, _, held, cols = d_ref.shape
    d = d_ref[:, 0].reshape(parts * held, cols).astype(F32)
    clip = lambda r: jnp.minimum(jnp.maximum(r, -huber_threshold), huber_threshold)

    def apply(high, low, v):
        vh, vl = split2(v)
        return mm(high[...], vh) + (mm(low[...], vh) + mm(high[...], vl))

    total = clip(d)
    for _ in range(ITERS - 1):
        total = total + clip(d - total + apply(k_hi, k_lo, total))
    series = apply(p_hi, p_lo, total)
    out[:, 0] = series.reshape(parts, series.shape[0] // parts, cols).astype(out.dtype)


def invert(sines, tables):
    parts, strips, held, cols = sines.shape
    mine = NDATES // parts
    fixed = [pl.BlockSpec(t.shape, lambda i: (0, 0)) for t in tables]
    n = parts * held
    return pl.pallas_call(
        invert_kernel,
        grid=(strips,),
        in_specs=[pl.BlockSpec((parts, 1, held, cols), lambda i: (0, i, 0, 0))] + fixed,
        out_specs=pl.BlockSpec((parts, 1, mine, cols), lambda i: (0, i, 0, 0)),
        out_shape=jax.ShapeDtypeStruct((parts, strips, mine, cols), BF),
        compiler_params=pltpu.CompilerParams(vmem_limit_bytes=32 << 20),
        cost_estimate=pl.CostEstimate(
            flops=6 * strips * cols * n * (2 * n + NDATES),
            bytes_accessed=4 * strips * cols * n,
            transcendentals=0,
        ),
        name="huber",
    )(sines, *tables)


def gauss_matrix(size_out, size_in, offset):
    distance = np.arange(size_in)[None, :] - offset - np.arange(size_out)[:, None]
    kernel = np.exp(-0.5 * (distance.astype(np.float32) / np.float32(blur_sigma)) ** 2)
    return np.where(np.abs(distance) <= RADIUS, kernel, 0.0).astype(np.float32)


def blur_kernel(halves, sel, *refs):
    owns, ones, twos = refs[:halves], refs[halves : 2 * halves], refs[2 * halves : 3 * halves]
    rk, ck_hi, ck_lo, inv_row, inv_col, corrected, atmosphere = refs[3 * halves :]
    group, rows, cols = corrected.shape
    pieces = []
    own = []
    for i in range(group):
        own.append(jnp.concatenate([o[i] for o in owns], axis=1))
        one = jnp.concatenate([o[i] for o in ones], axis=1)
        two = jnp.concatenate([o[i] for o in twos], axis=1)
        extended = jnp.concatenate(
            [pick(sel, one, two, 0, 1), own[i], pick(sel, one, two, 2, 3)], axis=0
        )
        both = mm(rk[...], extended)
        pieces.append((both[:rows] + both[rows:]).astype(BF))
    stacked = jnp.concatenate(pieces, axis=0)
    smooth = mm(stacked, ck_hi[...]) + mm(stacked, ck_lo[...])
    for i in range(group):
        air = smooth[i * rows : (i + 1) * rows] * inv_row[...] * inv_col[...]
        atmosphere[i] = air
        corrected[i] = own[i].astype(F32) - air


def blur(sel, owns, ones, twos):
    dates, rows, _ = owns[0].shape
    cols = sum(o.shape[2] for o in owns)
    halves = len(owns)
    group = next(g for g in (8, 5, 4, 2, 1) if dates % g == 0)
    hi = lambda v: v.astype(BF)
    lo = lambda v: (v - v.astype(BF).astype(np.float32)).astype(BF)
    row_filter = gauss_matrix(rows, rows + 2 * RADIUS, RADIUS)
    col_filter = gauss_matrix(cols, cols, 0)
    row_tables = jnp.asarray(np.concatenate([hi(row_filter), lo(row_filter)], axis=0))
    source = lax.axis_index("row") * rows - RADIUS + jnp.arange(rows + 2 * RADIUS, dtype=jnp.int32)
    inside = (source >= 0) & (source < rows * lax.axis_size("row"))
    row_weight = jnp.sum(jnp.where(inside[None, :], jnp.asarray(row_filter), 0.0), axis=1)
    fixed = [
        row_tables,
        jnp.asarray(hi(col_filter)),
        jnp.asarray(lo(col_filter)),
        (1.0 / row_weight)[:, None],
        jnp.asarray(1.0 / col_filter.sum(axis=0, dtype=np.float32))[None, :],
    ]
    block = pl.BlockSpec((group, rows, cols), lambda i: (i, 0, 0))
    cut = lambda v: pl.BlockSpec((group,) + v.shape[1:], lambda i: (i, 0, 0))
    arrays = [*owns, *ones, *twos]
    return pl.pallas_call(
        functools.partial(blur_kernel, halves),
        grid=(dates // group,),
        in_specs=[pl.BlockSpec(memory_space=pltpu.SMEM)]
        + [cut(v) for v in arrays]
        + [pl.BlockSpec(t.shape, lambda i: (0, 0)) for t in fixed],
        out_specs=[block, block],
        out_shape=[jax.ShapeDtypeStruct((dates, rows, cols), F32)] * 2,
        compiler_params=pltpu.CompilerParams(vmem_limit_bytes=50 << 20),
        name="blur",
    )(sel, *arrays, *fixed)


def exchange(top, bottom):
    n = lax.axis_size("row")
    even = lax.axis_index("row") % 2 == 0
    received = []
    for first, mine in ((0, jnp.where(even, bottom, top)), (1, jnp.where(even, top, bottom))):
        partner = list(range(n))
        for i in range(first, n - 1, 2):
            partner[i], partner[i + 1] = i + 1, i
        received.append(lax.ppermute(mine, "row", list(enumerate(partner))))
    return received


def sources():
    n, at = lax.axis_size("row"), lax.axis_index("row")
    even = at % 2 == 0
    flags = [~even, even & (at > 0), even & (at < n - 1), ~even & (at < n - 1)]
    return jnp.stack(flags).astype(jnp.int32)


def on_device(ifg_real, ifg_imag, date_pairs):
    count, rows, cols = ifg_real.shape
    parts = lax.axis_size("ifg")
    strip = rows // parts
    width = cols // 2
    cut = width + 128
    tables = spectral_tables(rows)
    groups = [(0, 8), (8, count - 8)] if count > 8 else [(0, count)]
    halos = []
    for at, size in groups:
        joined = jnp.stack([v[at : at + size, :, :cut] for v in (ifg_real, ifg_imag)])
        halos.append(exchange(joined[:, :, :HALF], joined[:, :, rows - HALF :]))
    joined = jnp.stack([v[:, :, cut:] for v in (ifg_real, ifg_imag)])
    more = exchange(joined[:, :, :HALF], joined[:, :, rows - HALF :])
    sel = sources()
    solver = inverse_tables(date_pairs)
    gate, *solver = lax.optimization_barrier((sel, *solver))

    def sines_of(n, gate, first, extra):
        at, size = groups[n]
        return filtered_sines(
            ifg_real, ifg_imag, gate, halos[n], extra, tables, at, size, first, width
        )

    def send(pieces):
        sines = jnp.concatenate(pieces, axis=0) if len(pieces) > 1 else pieces[0]
        sines = sines.reshape(count, parts, strip, width).transpose(1, 2, 0, 3)
        return lax.all_to_all(sines, "ifg", split_axis=0, concat_axis=0, tiled=True)

    def give(series):
        values = lax.all_to_all(series, "ifg", split_axis=0, concat_axis=0, tiled=True)
        values = values.transpose(2, 0, 1, 3).reshape(NDATES // parts, rows, width)
        one, two = exchange(values[:, :RADIUS], values[:, rows - RADIUS :])
        return values, one, two

    skipped = width // 128 - 1
    left = send([sines_of(n, gate, 0, ()) for n in range(len(groups))])
    right = [sines_of(0, gate, skipped, more)]
    series = invert(left, solver)
    gate, series = lax.optimization_barrier((gate, series))
    halves = [give(series)]
    right += [sines_of(n, gate, skipped, more) for n in range(1, len(groups))]
    halves.append(give(invert(send(right), solver)))
    return tuple(blur(sel, *zip(*halves)))


def solution(mesh):
    placed = (P("ifg", "row", None), P("ifg", "row", None), P())
    return jax.shard_map(
        on_device,
        mesh=mesh,
        in_specs=placed,
        out_specs=(P("ifg", "row", None), P("ifg", "row", None)),
        check_vma=False,
    )
```

time: 237 us -> 206 us (0.87)
  Pallas kernels: 118 us -> 88.1 us
  blocking collectives: 34.6 us -> 17.8 us
  waiting for transfers between devices: 29.4 us -> 34.6 us
  other arithmetic: 1.53 us -> 6.12 us
  local copies, waits for them, and re-layouts: 12.7 us -> 16.6 us
    pallas_call x4 -> x7, Pallas kernels: 112 us -> 81.6 us  [the longest x4 56.7 us: filtered_sines(): pl.pallas_call(functools.partial(filter_kernel, first, width, bool(more))...]
    all_to_all x1, blocking collectives: 34.6 us -> 17.8 us  [send(): return lax.all_to_all(sines, 'ifg', split_axis=0, concat_axis=0, tiled=True)]
    all_to_all x2 -> x3, waiting for transfers between devices: 8.79 us -> 24.8 us  [the longest x2 21.4 us: give(): lax.all_to_all(series, 'ifg', split_axis=0, concat_axis=0, tiled=True)]
    ppermute x10, waiting for transfers between devices: 20.6 us -> 9.83 us  [exchange(): received.append(lax.ppermute(mine, 'row', list(enumerate(partner))))]
    unnamed x33 -> x73, local copies, waits for them, and re-layouts: 2.01 us -> 8.21 us
    select_n x0 -> x5, other arithmetic: none -> 5.73 us  [exchange(): jnp.where(even, top, bottom)]
    slice x4 -> x0, local copies, waits for them, and re-layouts: 5.45 us -> none  [the longest x3 5.08 us: from_neighbours(): lax.slice_in_dim(block, 0, width, axis=dim)]
    reshape x4 -> x0, local copies, waits for them, and re-layouts: 4.9 us -> none  [the longest x2 3.1 us: on_device(): sines = sines.reshape(size, parts, strip, cols).transpose(1, 2, 0, 3)]
  transfers between devices with their start and end apart: 12 -> 13, of which waited for: 5 -> 5; matrix products, arithmetic and copies ran while one was open for 2% -> 6% of each run, Pallas kernels for 42% -> 25%
where the time goes in v2:
time: 206 us; the launch traced here: 204 us
  Pallas kernels  88.1 us (43%)
  starting transfers between devices  40.1 us (19%)
  waiting for transfers between devices  34.6 us (17%)
  blocking collectives  17.8 us (9%)
  local copies, waits for them, and re-layouts  16.6 us (8%)
  other arithmetic  6.12 us (3%)
    pallas_call x4, Pallas kernels, filtered_sines(): pl.pallas_call(functools.partial(filter_kernel, first, width, bool(more))...  56.7 us
    ppermute x10, starting transfers between devices, exchange(): received.append(lax.ppermute(mine, 'row', list(enumerate(partner))))  28.4 us
    all_to_all x2, waiting for transfers between devices, give(): lax.all_to_all(series, 'ifg', split_axis=0, concat_axis=0, tiled=True)  21.4 us
    all_to_all x1, blocking collectives, send(): return lax.all_to_all(sines, 'ifg', split_axis=0, concat_axis=0, tiled=True)  17.8 us
    pallas_call x2, Pallas kernels, invert(): pl.pallas_call(invert_kernel, grid=(strips,), in_specs=[pl.BlockSpec((par...  17.1 us
    ppermute x10, waiting for transfers between devices, exchange(): received.append(lax.ppermute(mine, 'row', list(enumerate(partner))))  9.83 us
    unnamed x73, local copies, waits for them, and re-layouts  8.21 us
    all_to_all x2, starting transfers between devices, give(): lax.all_to_all(series, 'ifg', split_axis=0, concat_axis=0, tiled=True)  7.99 us
  transfers between devices with their start and end apart: 13, of which 5 were waited for; matrix products, arithmetic and copies ran while one was open for 6% of the time, Pallas kernels for 25%

profile of v2, /device:TPU:0, one launch (start us, length us, event | category | flops | bytes accessed | tf_op | source)
XLA Modules:
  0.0 204.4 jit_solution(10517622932800793963)
XLA Ops:
  0.7 1.3 slice_bitcast_fusion.4
  2.0 1.1 broadcast_select_fusion.4
  3.1 4.5 %collective-permute-start.1 = (bf16[2,8,32,384]{3,2,1,0:T(8,128)(2,1)}, bf16[2,8,32,384]{3,2,1,0:T(8,128)(2,1)}, u32[]{:S(2)}, u32[]{:S(2)}) collective-permute-start(bf16[2,8,32,384]{3,2,1,0:T(8,128)(2,1)} %get-tuple-element.32), channel_id=1, source_target_pairs={{0,0},{1,2},{2,1},{3,3},{4,4},{5,6},{6,5},{7,7},{8,8},{9,10},{10,9... | collective-permute-start | bytes 1179656 | tf_op jit(solution)/shard_map/ppermute | solution.py:386
  7.5 2.1 %collective-permute-start = (bf16[2,8,32,384]{3,2,1,0:T(8,128)(2,1)}, bf16[2,8,32,384]{3,2,1,0:T(8,128)(2,1)}, u32[]{:S(2)}, u32[]{:S(2)}) collective-permute-start(bf16[2,8,32,384]{3,2,1,0:T(8,128)(2,1)} %get-tuple-element.33), channel_id=1, source_target_pairs={{0,1},{1,0},{2,3},{3,2},{4,5},{5,4},{6,7},{7,6},{8,9},{9,8},{10,11... | collective-permute-start | bytes 1179656 | tf_op jit(solution)/shard_map/ppermute | solution.py:386
  9.7 1.6 slice_bitcast_fusion
  11.3 1.7 broadcast_select_fusion
  13.0 1.9 collective-permute-start.3
  14.9 4.1 %collective-permute-start.2 = (bf16[2,24,32,384]{3,2,1,0:T(8,128)(2,1)}, bf16[2,24,32,384]{3,2,1,0:T(8,128)(2,1)}, u32[]{:S(2)}, u32[]{:S(2)}) collective-permute-start(bf16[2,24,32,384]{3,2,1,0:T(8,128)(2,1)} %get-tuple-element.25), channel_id=1, source_target_pairs={{0,1},{1,0},{2,3},{3,2},{4,5},{5,4},{6,7},{7,6},{8,9},{9,8},{10,11... | collective-permute-start | bytes 3538952 | tf_op jit(solution)/shard_map/ppermute | solution.py:386
  19.0 1.2 slice_bitcast_fusion.2
  20.3 0.0 copy-start.8
  20.3 1.2 broadcast_select_fusion.2
  21.5 5.4 %collective-permute-start.5 = (bf16[2,32,32,128]{3,2,1,0:T(8,128)(2,1)}, bf16[2,32,32,128]{3,2,1,0:T(8,128)(2,1)}, u32[]{:S(2)}, u32[]{:S(2)}) collective-permute-start(bf16[2,32,32,128]{3,2,1,0:T(8,128)(2,1)} %get-tuple-element.30), channel_id=1, source_target_pairs={{0,0},{1,2},{2,1},{3,3},{4,4},{5,6},{6,5},{7,7},{8,8},{9,10},{10,9... | collective-permute-start | bytes 1572872 | tf_op jit(solution)/shard_map/ppermute | solution.py:386
  26.9 0.1 copy.21.pairs
  27.0 0.1 add_convert_fusion.sel
  27.1 0.0 copy-start.18
  27.1 0.0 copy-start.21
  27.1 6.4 %newton.1 = (bf16[256,256]{1,0:T(8,128)(2,1)S(1)}, bf16[256,256]{1,0:T(8,128)(2,1)S(1)}, bf16[320,256]{1,0:T(8,128)(2,1)S(1)}, bf16[320,256]{1,0:T(8,128)(2,1)S(1)}) custom-call(s32[256,2]{1,0:T(8,128)S(1)} %copy.21.pairs, s32[2,256]{1,0:T(2,128)S(1)} %bitcast.35), custom_call_target="tpu_custom_call" | custom-call | flops 3221225472 | bytes 524288 | tf_op jit(solution)/shard_map/newton/pallas_call | solution.py:262
  33.6 0.1 collective-permute-start.4
  33.7 0.0 collective-permute-done.one
  33.8 7.7 %goldstein.4 = bf16[8,64,256]{2,1,0:T(8,128)(2,1)S(1)} custom-call(s32[4]{0:T(128)S(1)} %add_convert_fusion.sel, bf16[32,64,512]{2,1,0:T(8,128)(2,1)S(1)} %copy-done, bf16[32,64,512]{2,1,0:T(8,128)(2,1)S(1)} %copy-done.1, bf16[2,8,32,384]{3,2,1,0:T(8,128)(2,1)} %collective-permute-done.one, bf16[2,8,32,384]{3,2,1,0:T(8,128)(2,1)} %collective-permute-done.1.two, ...), custom_call_target="tpu_custom_call" | custom-call | flops 6144000000 | bytes 1048576 | tf_op jit(solution)/shard_map/goldstein/pallas_call | solution.py:205
  41.5 4.7 %collective-permute-done.2.one = bf16[2,24,32,384]{3,2,1,0:T(8,128)(2,1)} collective-permute-done((bf16[2,24,32,384]{3,2,1,0:T(8,128)(2,1)}, bf16[2,24,32,384]{3,2,1,0:T(8,128)(2,1)}, u32[]{:S(2)}, u32[]{:S(2)}) %collective-permute-start.2) | collective-permute-done | bytes 1179680 | tf_op jit(solution)/shard_map/ppermute | solution.py:386
  46.2 20.7 %goldstein.5 = bf16[24,64,256]{2,1,0:T(8,128)(2,1)S(1)} custom-call(s32[4]{0:T(128)S(1)} %add_convert_fusion.sel, bf16[32,64,512]{2,1,0:T(8,128)(2,1)S(1)} %copy-done, bf16[32,64,512]{2,1,0:T(8,128)(2,1)S(1)} %copy-done.1, bf16[2,24,32,384]{3,2,1,0:T(8,128)(2,1)} %collective-permute-done.2.one, bf16[2,24,32,384]{3,2,1,0:T(8,128)(2,1)S(1)} %collective-permute-done.3.two, ...), custom_call_target="tpu_custom_call" | custom-call | flops 18432000000 | bytes 3145728 | tf_op jit(solution)/shard_map/goldstein/pallas_call | solution.py:205
  66.9 0.1 pad_maximum_fusion.1
  67.0 1.6 copy.22
  68.5 3.7 %all-to-all-start = ((bf16[8,8,32,256]{3,2,1,0:T(8,128)(2,1)}), bf16[8,8,32,256]{3,2,1,0:T(8,128)(2,1)S(1)}, u32[]{:S(2)}, u32[]{:S(2)}) async-start(bf16[8,8,32,256]{3,2,1,0:T(8,128)(2,1)} %bitcast.39), calls=%async_computation | async-start | bytes 2097152 | tf_op jit(solution)/shard_map/all_to_all | solution.py:424
  72.3 0.0 copy-start.2
  72.3 1.6 copy-done.2
  73.9 0.9 copy-done.12
  74.8 0.9 copy-done.16
  75.7 0.9 copy-done.19
  76.6 7.7 %goldstein.6 = bf16[8,64,256]{2,1,0:T(8,128)(2,1)S(1)} custom-call(s32[4]{0:T(128)S(1)} %add_convert_fusion.sel, bf16[32,64,512]{2,1,0:T(8,128)(2,1)S(1)} %copy-done, bf16[32,64,512]{2,1,0:T(8,128)(2,1)S(1)} %copy-done.2, bf16[2,8,32,384]{3,2,1,0:T(8,128)(2,1)} %collective-permute-done.one, bf16[2,8,32,384]{3,2,1,0:T(8,128)(2,1)} %collective-permute-done.1.two, ...), custom_call_target="tpu_custom_call" | custom-call | flops 6144000000 | bytes 1048576 | tf_op jit(solution)/shard_map/goldstein/pallas_call | solution.py:205
  84.2 3.4 %all-to-all-done.d_ref = bf16[8,8,32,256]{3,2,1,0:T(8,128)(2,1)S(1)} async-done(((bf16[8,8,32,256]{3,2,1,0:T(8,128)(2,1)}), bf16[8,8,32,256]{3,2,1,0:T(8,128)(2,1)S(1)}, u32[]{:S(2)}, u32[]{:S(2)}) %all-to-all-start) | async-done | bytes 1048608 | tf_op jit(solution)/shard_map/all_to_all | solution.py:424
  87.6 0.9 copy-done.23
  88.5 0.9 copy-done.26
  89.5 0.9 copy-done.29
  90.4 0.9 copy-done.32
  91.3 0.0 copy-start.20
  91.3 8.6 %huber.2 = bf16[8,8,40,256]{3,2,1,0:T(8,128)(2,1)} custom-call(bf16[8,8,32,256]{3,2,1,0:T(8,128)(2,1)S(1)} %all-to-all-done.d_ref, bf16[256,256]{1,0:T(8,128)(2,1)S(1)} %copy-done.29, bf16[256,256]{1,0:T(8,128)(2,1)S(1)} %copy-done.32, bf16[320,256]{1,0:T(8,128)(2,1)S(1)} %copy-done.23, bf16[320,256]{1,0:T(8,128)(2,1)S(1)} %copy-done.26), custom_call_target="tpu_custom_call" | custom-call | flops 2617245696 | bytes 2097152 | tf_op jit(solution)/shard_map/huber/pallas_call | solution.py:297
  99.9 20.7 %goldstein.7 = bf16[24,64,256]{2,1,0:T(8,128)(2,1)S(1)} custom-call(s32[4]{0:T(128)S(1)} %add_convert_fusion.sel, bf16[32,64,512]{2,1,0:T(8,128)(2,1)S(1)} %copy-done, bf16[32,64,512]{2,1,0:T(8,128)(2,1)S(1)} %copy-done.3, bf16[2,24,32,384]{3,2,1,0:T(8,128)(2,1)} %collective-permute-done.2.one, bf16[2,24,32,384]{3,2,1,0:T(8,128)(2,1)S(1)} %copy-done.10, ...), custom_call_target="tpu_custom_call" | custom-call | flops 18432000000 | bytes 3145728 | tf_op jit(solution)/shard_map/goldstein/pallas_call | solution.py:205
  120.6 0.1 pad_maximum_fusion.2
  120.7 0.6 copy.24
  121.3 17.8 %all_to_all.20.d_ref = bf16[8,8,32,256]{3,2,1,0:T(8,128)(2,1)S(1)} all-to-all(bf16[8,8,32,256]{3,2,1,0:T(8,128)(2,1)S(1)} %bitcast.40), channel_id=1, replica_groups=mesh['ifg'=8,'row'=4] {'ifg'}, dimensions={0} | all-to-all | bytes 2097152 | tf_op jit(solution)/shard_map/all_to_all | solution.py:424
  139.1 3.7 %all-to-all-start.1 = ((bf16[8,8,40,256]{3,2,1,0:T(8,128)(2,1)}), bf16[8,8,40,256]{3,2,1,0:T(8,128)(2,1)S(1)}, u32[]{:S(2)}, u32[]{:S(2)}) async-start(bf16[8,8,40,256]{3,2,1,0:T(8,128)(2,1)} %huber.2), calls=%async_computation.1 | async-start | bytes 2621440 | tf_op jit(solution)/shard_map/all_to_all | solution.py:427
  142.8 8.6 %huber.3 = bf16[8,8,40,256]{3,2,1,0:T(8,128)(2,1)} custom-call(bf16[8,8,32,256]{3,2,1,0:T(8,128)(2,1)S(1)} %all_to_all.20.d_ref, bf16[256,256]{1,0:T(8,128)(2,1)S(1)} %copy-done.30, bf16[256,256]{1,0:T(8,128)(2,1)S(1)} %copy-done.33, bf16[320,256]{1,0:T(8,128)(2,1)S(1)} %copy-done.24, bf16[320,256]{1,0:T(8,128)(2,1)S(1)} %copy-done.27), custom_call_target="tpu_custom_call" | custom-call | flops 2617245696 | bytes 2097152 | tf_op jit(solution)/shard_map/huber/pallas_call | solution.py:297
  151.4 9.5 %all-to-all-done.1 = bf16[8,8,40,256]{3,2,1,0:T(8,128)(2,1)S(1)} async-done(((bf16[8,8,40,256]{3,2,1,0:T(8,128)(2,1)}), bf16[8,8,40,256]{3,2,1,0:T(8,128)(2,1)S(1)}, u32[]{:S(2)}, u32[]{:S(2)}) %all-to-all-start.1) | async-done | bytes 1310752 | tf_op jit(solution)/shard_map/all_to_all | solution.py:427
  160.9 4.3 %all-to-all-start.3 = ((bf16[8,8,40,256]{3,2,1,0:T(8,128)(2,1)}), bf16[8,8,40,256]{3,2,1,0:T(8,128)(2,1)}, u32[]{:S(2)}, u32[]{:S(2)}) async-start(bf16[8,8,40,256]{3,2,1,0:T(8,128)(2,1)} %huber.3), calls=%async_computation.3 | async-start | bytes 2621440 | tf_op jit(solution)/shard_map/all_to_all | solution.py:427
  165.2 0.3 copy.30
  165.5 0.9 broadcast_select_fusion.7
  166.4 1.6 collective-permute-start.8
  168.0 3.5 %collective-permute-start.6 = (bf16[40,16,256]{2,1,0:T(8,128)(2,1)}, bf16[40,16,256]{2,1,0:T(8,128)(2,1)S(1)}, u32[]{:S(2)}, u32[]{:S(2)}) collective-permute-start(bf16[40,16,256]{2,1,0:T(8,128)(2,1)} %get-tuple-element.29), channel_id=1, source_target_pairs={{0,1},{1,0},{2,3},{3,2},{4,5},{5,4},{6,7},{7,6},{8,9},{9,8},{10,11... | collective-permute-start | bytes 983048 | tf_op jit(solution)/shard_map/ppermute | solution.py:386
  171.5 11.9 %all-to-all-done.3 = bf16[8,8,40,256]{3,2,1,0:T(8,128)(2,1)} async-done(((bf16[8,8,40,256]{3,2,1,0:T(8,128)(2,1)}), bf16[8,8,40,256]{3,2,1,0:T(8,128)(2,1)}, u32[]{:S(2)}, u32[]{:S(2)}) %all-to-all-start.3) | async-done | bytes 1310752 | tf_op jit(solution)/shard_map/all_to_all | solution.py:427
  183.4 1.6 copy.29
  185.0 0.0 copy-start.35
  185.0 0.0 copy-start.4
  185.1 0.0 copy-start.5
  185.1 0.0 copy-start.6
  185.1 0.0 copy-start.7
  185.1 0.9 broadcast_select_fusion.6
  186.0 1.8 collective-permute-start.9
  187.7 3.5 %collective-permute-start.7 = (bf16[40,16,256]{2,1,0:T(8,128)(2,1)}, bf16[40,16,256]{2,1,0:T(8,128)(2,1)}, u32[]{:S(2)}, u32[]{:S(2)}) collective-permute-start(bf16[40,16,256]{2,1,0:T(8,128)(2,1)} %get-tuple-element.27), channel_id=1, source_target_pairs={{0,1},{1,0},{2,3},{3,2},{4,5},{5,4},{6,7},{7,6},{8,9},{9,8},{10,11... | collective-permute-start | bytes 983048 | tf_op jit(solution)/shard_map/ppermute | solution.py:386
  191.2 0.1 select_reduce_fusion
  191.4 0.1 copy.26.refs_9_
  191.5 5.1 %collective-permute-done.7.refs_3_ = bf16[40,16,256]{2,1,0:T(8,128)(2,1)} collective-permute-done((bf16[40,16,256]{2,1,0:T(8,128)(2,1)}, bf16[40,16,256]{2,1,0:T(8,128)(2,1)}, u32[]{:S(2)}, u32[]{:S(2)}) %collective-permute-start.7) | collective-permute-done | bytes 327712 | tf_op jit(solution)/shard_map/ppermute | solution.py:386
  196.6 7.8 %blur.1 = (f32[40,64,512]{2,1,0:T(8,128)}, f32[40,64,512]{2,1,0:T(8,128)}) custom-call(s32[4]{0:T(128)S(1)} %add_convert_fusion.sel, bf16[40,64,256]{2,1,0:T(8,128)(2,1)S(1)} %bitcast.34, bf16[40,64,256]{2,1,0:T(8,128)(2,1)} %bitcast.37, bf16[40,16,256]{2,1,0:T(8,128)(2,1)S(1)} %collective-permute-done.6.refs_2_, ...), custom_call_target="tpu_custom_call" | custom-call | tf_op jit(solution)/shard_map/blur/pallas_call | solution.py:365
  (63 shorter events, 0.1 us)
Async XLA Ops:
  0.6 9.0 %copy-start = (bf16[32,64,512]{2,1,0:T(8,128)(2,1)S(1)}, bf16[32,64,512]{2,1,0:T(8,128)(2,1)}, u32[]{:S(2)}) copy-start(bf16[32,64,512]{2,1,0:T(8,128)(2,1)} %re.7) | copy-start | bytes 6291460
  3.1 30.5 %collective-permute-start.1 = (bf16[2,8,32,384]{3,2,1,0:T(8,128)(2,1)}, bf16[2,8,32,384]{3,2,1,0:T(8,128)(2,1)}, u32[]{:S(2)}, u32[]{:S(2)}) collective-permute-start(bf16[2,8,32,384]{3,2,1,0:T(8,128)(2,1)} %get-tuple-element.32), channel_id=1, source_target_pairs={{0,0},{1,2},{2,1},{3,3},{4,4},{5,6},{6,5},{7,7},{8,8},{9,10},{10,9... | collective-permute-start | bytes 1179656 | tf_op jit(solution)/shard_map/ppermute | solution.py:386
  7.5 26.1 %collective-permute-start = (bf16[2,8,32,384]{3,2,1,0:T(8,128)(2,1)}, bf16[2,8,32,384]{3,2,1,0:T(8,128)(2,1)}, u32[]{:S(2)}, u32[]{:S(2)}) collective-permute-start(bf16[2,8,32,384]{3,2,1,0:T(8,128)(2,1)} %get-tuple-element.33), channel_id=1, source_target_pairs={{0,1},{1,0},{2,3},{3,2},{4,5},{5,4},{6,7},{7,6},{8,9},{9,8},{10,11... | collective-permute-start | bytes 1179656 | tf_op jit(solution)/shard_map/ppermute | solution.py:386
  13.0 28.5 %collective-permute-start.3 = (bf16[2,24,32,384]{3,2,1,0:T(8,128)(2,1)}, bf16[2,24,32,384]{3,2,1,0:T(8,128)(2,1)S(1)}, u32[]{:S(2)}, u32[]{:S(2)}) collective-permute-start(bf16[2,24,32,384]{3,2,1,0:T(8,128)(2,1)} %get-tuple-element.24), channel_id=1, source_target_pairs={{0,0},{1,2},{2,1},{3,3},{4,4},{5,6},{6,5},{7,7},{8,8},{9,10},{10,9... | collective-permute-start | bytes 3538952 | tf_op jit(solution)/shard_map/ppermute | solution.py:386
  14.9 31.3 %collective-permute-start.2 = (bf16[2,24,32,384]{3,2,1,0:T(8,128)(2,1)}, bf16[2,24,32,384]{3,2,1,0:T(8,128)(2,1)}, u32[]{:S(2)}, u32[]{:S(2)}) collective-permute-start(bf16[2,24,32,384]{3,2,1,0:T(8,128)(2,1)} %get-tuple-element.25), channel_id=1, source_target_pairs={{0,1},{1,0},{2,3},{3,2},{4,5},{5,4},{6,7},{7,6},{8,9},{9,8},{10,11... | collective-permute-start | bytes 3538952 | tf_op jit(solution)/shard_map/ppermute | solution.py:386
  20.3 6.6 %copy-start.8 = (s32[256,2]{0,1:T(2,128)S(1)}, s32[256,2]{0,1:T(2,128)}, u32[]{:S(2)}) copy-start(s32[256,2]{0,1:T(2,128)} %param.15) | copy-start | bytes 6148
  21.5 50.8 %collective-permute-start.5 = (bf16[2,32,32,128]{3,2,1,0:T(8,128)(2,1)}, bf16[2,32,32,128]{3,2,1,0:T(8,128)(2,1)}, u32[]{:S(2)}, u32[]{:S(2)}) collective-permute-start(bf16[2,32,32,128]{3,2,1,0:T(8,128)(2,1)} %get-tuple-element.30), channel_id=1, source_target_pairs={{0,0},{1,2},{2,1},{3,3},{4,4},{5,6},{6,5},{7,7},{8,8},{9,10},{10,9... | collective-permute-start | bytes 1572872 | tf_op jit(solution)/shard_map/ppermute | solution.py:386
  27.1 6.6 %copy-start.1 = (bf16[32,64,512]{2,1,0:T(8,128)(2,1)S(1)}, bf16[32,64,512]{2,1,0:T(8,128)(2,1)}, u32[]{:S(2)}) copy-start(bf16[32,64,512]{2,1,0:T(8,128)(2,1)} %im.7) | copy-start | bytes 6291460
  27.1 6.6 %copy-start.11 = (bf16[384,256]{1,0:T(8,128)(2,1)S(1)}, bf16[384,256]{1,0:T(8,128)(2,1)}, u32[]{:S(2)}) copy-start(bf16[384,256]{1,0:T(8,128)(2,1)} %constant.63.clone.refs_1_.refs_3_) | copy-start | bytes 589828
  27.1 6.6 %copy-start.14 = (bf16[256,256]{1,0:T(8,128)(2,1)S(1)}, bf16[256,256]{1,0:T(8,128)(2,1)}, u32[]{:S(2)}) copy-start(bf16[256,256]{1,0:T(8,128)(2,1)} %constant.65.clone.refs_3_.refs_5_) | copy-start | bytes 393220
  27.1 6.6 %copy-start.15 = (bf16[256,256]{1,0:T(8,128)(2,1)S(1)}, bf16[256,256]{1,0:T(8,128)(2,1)}, u32[]{:S(2)}) copy-start(bf16[256,256]{1,0:T(8,128)(2,1)} %constant.62.clone.refs_0_.refs_2_) | copy-start | bytes 393220
  27.1 6.6 %copy-start.18 = (bf16[128,384]{1,0:T(8,128)(2,1)S(1)}, bf16[128,384]{1,0:T(8,128)(2,1)}, u32[]{:S(2)}) copy-start(bf16[128,384]{1,0:T(8,128)(2,1)} %constant.64.clone.refs_2_.refs_4_) | copy-start | bytes 294916
  27.1 6.6 %copy-start.21 = (f32[1,256]{1,0:T(1,128)S(1)}, f32[1,256]{1,0:T(1,128)}, u32[]{:S(2)}) copy-start(f32[1,256]{1,0:T(1,128)} %constant.66.clone.refs_4_.refs_6_) | copy-start | bytes 3076
  33.6 7.9 %copy-start.22 = (bf16[320,256]{1,0:T(8,128)(2,1)}, bf16[320,256]{1,0:T(8,128)(2,1)S(1)}, u32[]{:S(2)}) copy-start(bf16[320,256]{1,0:T(8,128)(2,1)S(1)} %get-tuple-element.20.p_hi) | copy-start | bytes 491524
  33.6 7.9 %copy-start.25 = (bf16[320,256]{1,0:T(8,128)(2,1)}, bf16[320,256]{1,0:T(8,128)(2,1)S(1)}, u32[]{:S(2)}) copy-start(bf16[320,256]{1,0:T(8,128)(2,1)S(1)} %get-tuple-element.21.p_lo) | copy-start | bytes 491524
  33.6 7.9 %copy-start.28 = (bf16[256,256]{1,0:T(8,128)(2,1)}, bf16[256,256]{1,0:T(8,128)(2,1)S(1)}, u32[]{:S(2)}) copy-start(bf16[256,256]{1,0:T(8,128)(2,1)S(1)} %get-tuple-element.18.k_hi) | copy-start | bytes 393220
  33.6 7.9 %copy-start.31 = (bf16[256,256]{1,0:T(8,128)(2,1)}, bf16[256,256]{1,0:T(8,128)(2,1)S(1)}, u32[]{:S(2)}) copy-start(bf16[256,256]{1,0:T(8,128)(2,1)S(1)} %get-tuple-element.19.k_lo) | copy-start | bytes 393220
  33.6 38.7 %collective-permute-start.4 = (bf16[2,32,32,128]{3,2,1,0:T(8,128)(2,1)}, bf16[2,32,32,128]{3,2,1,0:T(8,128)(2,1)}, u32[]{:S(2)}, u32[]{:S(2)}) collective-permute-start(bf16[2,32,32,128]{3,2,1,0:T(8,128)(2,1)} %get-tuple-element.31), channel_id=1, source_target_pairs={{0,1},{1,0},{2,3},{3,2},{4,5},{5,4},{6,7},{7,6},{8,9},{9,8},{10,11... | collective-permute-start | bytes 1572872 | tf_op jit(solution)/shard_map/ppermute | solution.py:386
  41.5 25.4 %copy-start.9 = (bf16[2,24,32,384]{3,2,1,0:T(8,128)(2,1)}, bf16[2,24,32,384]{3,2,1,0:T(8,128)(2,1)S(1)}, u32[]{:S(2)}) copy-start(bf16[2,24,32,384]{3,2,1,0:T(8,128)(2,1)S(1)} %collective-permute-done.3.two) | copy-start | bytes 3538948
  68.5 19.1 %all-to-all-start = ((bf16[8,8,32,256]{3,2,1,0:T(8,128)(2,1)}), bf16[8,8,32,256]{3,2,1,0:T(8,128)(2,1)S(1)}, u32[]{:S(2)}, u32[]{:S(2)}) async-start(bf16[8,8,32,256]{3,2,1,0:T(8,128)(2,1)} %bitcast.39), calls=%async_computation | async-start | bytes 2097152 | tf_op jit(solution)/shard_map/all_to_all | solution.py:424
  72.3 1.6 copy-start.2
  73.9 0.9 copy-start.12
  74.8 0.9 copy-start.16
  75.7 0.9 copy-start.19
  87.6 0.9 copy-start.23
  88.5 0.9 copy-start.26
  89.5 0.9 copy-start.29
  90.4 0.9 copy-start.32
  91.3 8.6 %copy-start.3 = (bf16[32,64,512]{2,1,0:T(8,128)(2,1)S(1)}, bf16[32,64,512]{2,1,0:T(8,128)(2,1)}, u32[]{:S(2)}) copy-start(bf16[32,64,512]{2,1,0:T(8,128)(2,1)} %im.7) | copy-start | bytes 6291460
  91.3 8.6 %copy-start.10 = (bf16[2,24,32,384]{3,2,1,0:T(8,128)(2,1)S(1)}, bf16[2,24,32,384]{3,2,1,0:T(8,128)(2,1)}, u32[]{:S(2)}) copy-start(bf16[2,24,32,384]{3,2,1,0:T(8,128)(2,1)} %copy-done.9) | copy-start | bytes 3538948
  91.3 8.6 %copy-start.13 = (bf16[384,256]{1,0:T(8,128)(2,1)S(1)}, bf16[384,256]{1,0:T(8,128)(2,1)}, u32[]{:S(2)}) copy-start(bf16[384,256]{1,0:T(8,128)(2,1)} %constant.63.clone.refs_1_.refs_3_) | copy-start | bytes 589828
  91.3 8.6 %copy-start.17 = (bf16[256,256]{1,0:T(8,128)(2,1)S(1)}, bf16[256,256]{1,0:T(8,128)(2,1)}, u32[]{:S(2)}) copy-start(bf16[256,256]{1,0:T(8,128)(2,1)} %constant.62.clone.refs_0_.refs_2_) | copy-start | bytes 393220
  91.3 8.6 %copy-start.20 = (bf16[128,384]{1,0:T(8,128)(2,1)S(1)}, bf16[128,384]{1,0:T(8,128)(2,1)}, u32[]{:S(2)}) copy-start(bf16[128,384]{1,0:T(8,128)(2,1)} %constant.64.clone.refs_2_.refs_4_) | copy-start | bytes 294916
  139.1 3.7 %copy-start.24 = (bf16[320,256]{1,0:T(8,128)(2,1)S(1)}, bf16[320,256]{1,0:T(8,128)(2,1)}, u32[]{:S(2)}) copy-start(bf16[320,256]{1,0:T(8,128)(2,1)} %copy-done.22) | copy-start | bytes 491524
  139.1 3.7 %copy-start.27 = (bf16[320,256]{1,0:T(8,128)(2,1)S(1)}, bf16[320,256]{1,0:T(8,128)(2,1)}, u32[]{:S(2)}) copy-start(bf16[320,256]{1,0:T(8,128)(2,1)} %copy-done.25) | copy-start | bytes 491524
  139.1 3.8 %copy-start.30 = (bf16[256,256]{1,0:T(8,128)(2,1)S(1)}, bf16[256,256]{1,0:T(8,128)(2,1)}, u32[]{:S(2)}) copy-start(bf16[256,256]{1,0:T(8,128)(2,1)} %copy-done.28) | copy-start | bytes 393220
  139.1 3.8 %copy-start.33 = (bf16[256,256]{1,0:T(8,128)(2,1)S(1)}, bf16[256,256]{1,0:T(8,128)(2,1)}, u32[]{:S(2)}) copy-start(bf16[256,256]{1,0:T(8,128)(2,1)} %copy-done.31) | copy-start | bytes 393220
  139.1 21.8 %all-to-all-start.1 = ((bf16[8,8,40,256]{3,2,1,0:T(8,128)(2,1)}), bf16[8,8,40,256]{3,2,1,0:T(8,128)(2,1)S(1)}, u32[]{:S(2)}, u32[]{:S(2)}) async-start(bf16[8,8,40,256]{3,2,1,0:T(8,128)(2,1)} %huber.2), calls=%async_computation.1 | async-start | bytes 2621440 | tf_op jit(solution)/shard_map/all_to_all | solution.py:427
  160.9 22.5 %all-to-all-start.3 = ((bf16[8,8,40,256]{3,2,1,0:T(8,128)(2,1)}), bf16[8,8,40,256]{3,2,1,0:T(8,128)(2,1)}, u32[]{:S(2)}, u32[]{:S(2)}) async-start(bf16[8,8,40,256]{3,2,1,0:T(8,128)(2,1)} %huber.3), calls=%async_computation.3 | async-start | bytes 2621440 | tf_op jit(solution)/shard_map/all_to_all | solution.py:427
  166.4 25.0 %collective-permute-start.8 = (bf16[40,16,256]{2,1,0:T(8,128)(2,1)}, bf16[40,16,256]{2,1,0:T(8,128)(2,1)S(1)}, u32[]{:S(2)}, u32[]{:S(2)}) collective-permute-start(bf16[40,16,256]{2,1,0:T(8,128)(2,1)} %get-tuple-element.28), channel_id=1, source_target_pairs={{0,0},{1,2},{2,1},{3,3},{4,4},{5,6},{6,5},{7,7},{8,8},{9,10},{10,9... | collective-permute-start | bytes 983048 | tf_op jit(solution)/shard_map/ppermute | solution.py:386
  168.0 23.4 %collective-permute-start.6 = (bf16[40,16,256]{2,1,0:T(8,128)(2,1)}, bf16[40,16,256]{2,1,0:T(8,128)(2,1)S(1)}, u32[]{:S(2)}, u32[]{:S(2)}) collective-permute-start(bf16[40,16,256]{2,1,0:T(8,128)(2,1)} %get-tuple-element.29), channel_id=1, source_target_pairs={{0,1},{1,0},{2,3},{3,2},{4,5},{5,4},{6,7},{7,6},{8,9},{9,8},{10,11... | collective-permute-start | bytes 983048 | tf_op jit(solution)/shard_map/ppermute | solution.py:386
  185.0 6.3 %copy-start.34 = (bf16[40,8,8,256]{3,2,1,0:T(8,128)(2,1)}, bf16[40,8,8,256]{3,2,1,0:T(8,128)(2,1)S(1)}, u32[]{:S(2)}) copy-start(bf16[40,8,8,256]{3,2,1,0:T(8,128)(2,1)S(1)} %copy.29) | copy-start | bytes 3932164
  185.0 6.2 %copy-start.35 = (f32[64,96]{1,0:T(8,128)S(1)}, f32[64,96]{1,0:T(8,128)}, u32[]{:S(2)}) copy-start(f32[64,96]{1,0:T(8,128)} %constant.68.clone) | copy-start | bytes 73732
  185.0 11.6 %copy-start.4 = (bf16[512,512]{1,0:T(8,128)(2,1)S(1)}, bf16[512,512]{1,0:T(8,128)(2,1)}, u32[]{:S(2)}) copy-start(bf16[512,512]{1,0:T(8,128)(2,1)} %constant.70.clone.refs_8_) | copy-start | bytes 1572868
  185.1 11.5 %copy-start.5 = (bf16[512,512]{1,0:T(8,128)(2,1)S(1)}, bf16[512,512]{1,0:T(8,128)(2,1)}, u32[]{:S(2)}) copy-start(bf16[512,512]{1,0:T(8,128)(2,1)} %constant.69.clone.refs_7_) | copy-start | bytes 1572868
  185.1 11.5 %copy-start.6 = (bf16[128,96]{1,0:T(8,128)(2,1)S(1)}, bf16[128,96]{1,0:T(8,128)(2,1)}, u32[]{:S(2)}) copy-start(bf16[128,96]{1,0:T(8,128)(2,1)} %constant.67.clone.refs_6_) | copy-start | bytes 73732
  185.1 11.5 %copy-start.7 = (f32[1,512]{1,0:T(1,128)S(1)}, f32[1,512]{1,0:T(1,128)}, u32[]{:S(2)}) copy-start(f32[1,512]{1,0:T(1,128)} %constant.72.refs_10_) | copy-start | bytes 6148
  186.0 5.5 %collective-permute-start.9 = (bf16[40,16,256]{2,1,0:T(8,128)(2,1)}, bf16[40,16,256]{2,1,0:T(8,128)(2,1)S(1)}, u32[]{:S(2)}, u32[]{:S(2)}) collective-permute-start(bf16[40,16,256]{2,1,0:T(8,128)(2,1)} %get-tuple-element.26), channel_id=1, source_target_pairs={{0,0},{1,2},{2,1},{3,3},{4,4},{5,6},{6,5},{7,7},{8,8},{9,10},{10,9... | collective-permute-start | bytes 983048 | tf_op jit(solution)/shard_map/ppermute | solution.py:386
  187.7 8.8 %collective-permute-start.7 = (bf16[40,16,256]{2,1,0:T(8,128)(2,1)}, bf16[40,16,256]{2,1,0:T(8,128)(2,1)}, u32[]{:S(2)}, u32[]{:S(2)}) collective-permute-start(bf16[40,16,256]{2,1,0:T(8,128)(2,1)} %get-tuple-element.27), channel_id=1, source_target_pairs={{0,1},{1,0},{2,3},{3,2},{4,5},{5,4},{6,7},{7,6},{8,9},{9,8},{10,11... | collective-permute-start | bytes 983048 | tf_op jit(solution)/shard_map/ppermute | solution.py:386

commit v3 on v2

--- a/solution.py
+++ b/solution.py
@@ -8,6 +8,7 @@
 from jax.experimental import pallas as pl
 from jax.experimental.pallas import tpu as pltpu
 from jax.sharding import PartitionSpec as P
+
 
 PATCH = 64
 HALF = PATCH // 2
@@ -98,7 +99,7 @@
     if split:
         one_more, two_more, *refs = refs
     cf, rf, ri, ci, tp, out, pad_re, pad_im, even_re, even_im, odd_re, odd_im = refs
-    group, rows, cols = re.shape
+    group, rows, _ = re.shape
     extended = rows + PATCH
     window = width + 128
     start = 128 * first
@@ -279,8 +280,8 @@
     clip = lambda r: jnp.minimum(jnp.maximum(r, -huber_threshold), huber_threshold)
 
     def apply(high, low, v):
-        vh, vl = split2(v)
-        return mm(high[...], vh) + (mm(low[...], vh) + mm(high[...], vl))
+        v = v.astype(BF)
+        return mm(high[...], v) + mm(low[...], v)
 
     total = clip(d)
     for _ in range(ITERS - 1):
@@ -319,7 +320,7 @@
 def blur_kernel(halves, sel, *refs):
     owns, ones, twos = refs[:halves], refs[halves : 2 * halves], refs[2 * halves : 3 * halves]
     rk, ck_hi, ck_lo, inv_row, inv_col, corrected, atmosphere = refs[3 * halves :]
-    group, rows, cols = corrected.shape
+    group, rows, _ = corrected.shape
     pieces = []
     own = []
     for i in range(group):
@@ -424,7 +425,9 @@
         return lax.all_to_all(sines, "ifg", split_axis=0, concat_axis=0, tiled=True)
 
     def give(series):
-        values = lax.all_to_all(series, "ifg", split_axis=0, concat_axis=0, tiled=True)
+        return lax.all_to_all(series, "ifg", split_axis=0, concat_axis=0, tiled=True)
+
+    def bordered(values):
         values = values.transpose(2, 0, 1, 3).reshape(NDATES // parts, rows, width)
         one, two = exchange(values[:, :RADIUS], values[:, rows - RADIUS :])
         return values, one, two
@@ -434,14 +437,17 @@
     right = [sines_of(0, gate, skipped, more)]
     series = invert(left, solver)
     gate, series = lax.optimization_barrier((gate, series))
-    halves = [give(series)]
+    out_left = give(series)
     right += [sines_of(n, gate, skipped, more) for n in range(1, len(groups))]
-    halves.append(give(invert(send(right), solver)))
+    *right, out_left = lax.optimization_barrier((*right, out_left))
+    out_right = give(invert(send(right), solver))
+    halves = [bordered(out_left), bordered(out_right)]
     return tuple(blur(sel, *zip(*halves)))
 
 
 def solution(mesh):
     placed = (P("ifg", "row", None), P("ifg", "row", None), P())
+
     return jax.shard_map(
         on_device,
         mesh=mesh,

time: 206 us -> 200 us (0.971)
  waiting for transfers between devices: 34.6 us -> 23.8 us
  local copies, waits for them, and re-layouts: 16.6 us -> 22.5 us
  Pallas kernels: 88.1 us -> 84.8 us
    all_to_all x2, waiting for transfers between devices: 21.4 us -> 10.6 us  [give(): lax.all_to_all(series, 'ifg', split_axis=0, concat_axis=0, tiled=True)]
    unnamed x73, local copies, waits for them, and re-layouts: 8.21 us -> 12.9 us
    pallas_call x2, Pallas kernels: 17.1 us -> 13.9 us  [invert(): pl.pallas_call(invert_kernel, grid=(strips,), in_specs=[pl.BlockSpec((par...]
  transfers between devices with their start and end apart: 13 -> 13, of which waited for: 5 -> 4; matrix products, arithmetic and copies ran while one was open for 6% -> 6% of each run, Pallas kernels for 25% -> 32%
where the time goes in v3:
time: 200 us; the launch traced here: 199 us
  Pallas kernels  84.8 us (42%)
  starting transfers between devices  40.8 us (20%)
  waiting for transfers between devices  23.8 us (12%)
  local copies, waits for them, and re-layouts  22.5 us (11%)
  blocking collectives  19.4 us (10%)
  other arithmetic  6.13 us (3%)
    pallas_call x4, Pallas kernels, filtered_sines(): pl.pallas_call(functools.partial(filter_kernel, first, width, bool(more))...  56.7 us
    ppermute x10, starting transfers between devices, exchange(): received.append(lax.ppermute(mine, 'row', list(enumerate(partner))))  28.4 us
    all_to_all x1, blocking collectives, send(): return lax.all_to_all(sines, 'ifg', split_axis=0, concat_axis=0, tiled=True)  19.4 us
    pallas_call x2, Pallas kernels, invert(): pl.pallas_call(invert_kernel, grid=(strips,), in_specs=[pl.BlockSpec((par...  13.9 us
    unnamed x73, local copies, waits for them, and re-layouts  12.9 us
    all_to_all x2, waiting for transfers between devices, give(): lax.all_to_all(series, 'ifg', split_axis=0, concat_axis=0, tiled=True)  10.6 us
    ppermute x10, waiting for transfers between devices, exchange(): received.append(lax.ppermute(mine, 'row', list(enumerate(partner))))  9.8 us
    all_to_all x2, starting transfers between devices, give(): lax.all_to_all(series, 'ifg', split_axis=0, concat_axis=0, tiled=True)  8.67 us
  transfers between devices with their start and end apart: 13, of which 4 were waited for; matrix products, arithmetic and copies ran while one was open for 6% of the time, Pallas kernels for 32%

profile of v3, /device:TPU:0, one launch (start us, length us, event | category | flops | bytes accessed | tf_op | source)
XLA Modules:
  0.0 198.5 jit_solution(17588066589747407607)
XLA Ops:
  0.7 1.3 slice_bitcast_fusion.4
  2.0 1.1 broadcast_select_fusion.4
  3.1 4.5 %collective-permute-start.1 = (bf16[2,8,32,384]{3,2,1,0:T(8,128)(2,1)}, bf16[2,8,32,384]{3,2,1,0:T(8,128)(2,1)}, u32[]{:S(2)}, u32[]{:S(2)}) collective-permute-start(bf16[2,8,32,384]{3,2,1,0:T(8,128)(2,1)} %get-tuple-element.38), channel_id=1, source_target_pairs={{0,0},{1,2},{2,1},{3,3},{4,4},{5,6},{6,5},{7,7},{8,8},{9,10},{10,9... | collective-permute-start | bytes 1179656 | tf_op jit(solution)/shard_map/ppermute | solution.py:387
  7.6 2.1 %collective-permute-start = (bf16[2,8,32,384]{3,2,1,0:T(8,128)(2,1)}, bf16[2,8,32,384]{3,2,1,0:T(8,128)(2,1)}, u32[]{:S(2)}, u32[]{:S(2)}) collective-permute-start(bf16[2,8,32,384]{3,2,1,0:T(8,128)(2,1)} %get-tuple-element.39), channel_id=1, source_target_pairs={{0,1},{1,0},{2,3},{3,2},{4,5},{5,4},{6,7},{7,6},{8,9},{9,8},{10,11... | collective-permute-start | bytes 1179656 | tf_op jit(solution)/shard_map/ppermute | solution.py:387
  9.7 1.6 slice_bitcast_fusion
  11.3 1.7 broadcast_select_fusion
  13.0 1.9 collective-permute-start.5
  14.9 4.2 %collective-permute-start.4 = (bf16[2,24,32,384]{3,2,1,0:T(8,128)(2,1)}, bf16[2,24,32,384]{3,2,1,0:T(8,128)(2,1)}, u32[]{:S(2)}, u32[]{:S(2)}) collective-permute-start(bf16[2,24,32,384]{3,2,1,0:T(8,128)(2,1)} %get-tuple-element.31), channel_id=1, source_target_pairs={{0,1},{1,0},{2,3},{3,2},{4,5},{5,4},{6,7},{7,6},{8,9},{9,8},{10,11... | collective-permute-start | bytes 3538952 | tf_op jit(solution)/shard_map/ppermute | solution.py:387
  19.1 1.2 slice_bitcast_fusion.2
  20.3 1.3 broadcast_select_fusion.2
  21.5 5.4 %collective-permute-start.3 = (bf16[2,32,32,128]{3,2,1,0:T(8,128)(2,1)}, bf16[2,32,32,128]{3,2,1,0:T(8,128)(2,1)}, u32[]{:S(2)}, u32[]{:S(2)}) collective-permute-start(bf16[2,32,32,128]{3,2,1,0:T(8,128)(2,1)} %get-tuple-element.36), channel_id=1, source_target_pairs={{0,0},{1,2},{2,1},{3,3},{4,4},{5,6},{6,5},{7,7},{8,8},{9,10},{10,9... | collective-permute-start | bytes 1572872 | tf_op jit(solution)/shard_map/ppermute | solution.py:387
  26.9 0.1 copy.21.pairs
  27.1 0.1 add_convert_fusion.sel
  27.1 0.0 copy-start.18
  27.2 0.0 copy-start.21
  27.2 6.4 %newton.1 = (bf16[256,256]{1,0:T(8,128)(2,1)S(1)}, bf16[256,256]{1,0:T(8,128)(2,1)S(1)}, bf16[320,256]{1,0:T(8,128)(2,1)S(1)}, bf16[320,256]{1,0:T(8,128)(2,1)S(1)}) custom-call(s32[256,2]{1,0:T(8,128)S(1)} %copy.21.pairs, s32[2,256]{1,0:T(2,128)S(1)} %bitcast.35), custom_call_target="tpu_custom_call" | custom-call | flops 3221225472 | bytes 524288 | tf_op jit(solution)/shard_map/newton/pallas_call | solution.py:263
  33.7 0.1 collective-permute-start.2
  33.8 7.7 %goldstein.5 = bf16[8,64,256]{2,1,0:T(8,128)(2,1)S(1)} custom-call(s32[4]{0:T(128)S(1)} %add_convert_fusion.sel, bf16[32,64,512]{2,1,0:T(8,128)(2,1)S(1)} %copy-done, bf16[32,64,512]{2,1,0:T(8,128)(2,1)S(1)} %copy-done.1, bf16[2,8,32,384]{3,2,1,0:T(8,128)(2,1)} %collective-permute-done.one, bf16[2,8,32,384]{3,2,1,0:T(8,128)(2,1)} %collective-permute-done.1.two, ...), custom_call_target="tpu_custom_call" | custom-call | flops 6144000000 | bytes 1048576 | tf_op jit(solution)/shard_map/goldstein/pallas_call | solution.py:206
  41.5 4.7 %collective-permute-done.4.one = bf16[2,24,32,384]{3,2,1,0:T(8,128)(2,1)} collective-permute-done((bf16[2,24,32,384]{3,2,1,0:T(8,128)(2,1)}, bf16[2,24,32,384]{3,2,1,0:T(8,128)(2,1)}, u32[]{:S(2)}, u32[]{:S(2)}) %collective-permute-start.4) | collective-permute-done | bytes 1179680 | tf_op jit(solution)/shard_map/ppermute | solution.py:387
  46.2 20.7 %goldstein.6 = bf16[24,64,256]{2,1,0:T(8,128)(2,1)S(1)} custom-call(s32[4]{0:T(128)S(1)} %add_convert_fusion.sel, bf16[32,64,512]{2,1,0:T(8,128)(2,1)S(1)} %copy-done, bf16[32,64,512]{2,1,0:T(8,128)(2,1)S(1)} %copy-done.1, bf16[2,24,32,384]{3,2,1,0:T(8,128)(2,1)} %collective-permute-done.4.one, bf16[2,24,32,384]{3,2,1,0:T(8,128)(2,1)S(1)} %collective-permute-done.5.two, ...), custom_call_target="tpu_custom_call" | custom-call | flops 18432000000 | bytes 3145728 | tf_op jit(solution)/shard_map/goldstein/pallas_call | solution.py:206
  66.9 0.1 pad_maximum_fusion.1
  67.0 1.6 copy.22
  68.6 3.7 %all-to-all-start = ((bf16[8,8,32,256]{3,2,1,0:T(8,128)(2,1)}), bf16[8,8,32,256]{3,2,1,0:T(8,128)(2,1)S(1)}, u32[]{:S(2)}, u32[]{:S(2)}) async-start(bf16[8,8,32,256]{3,2,1,0:T(8,128)(2,1)} %bitcast.38), calls=%async_computation | async-start | bytes 2097152 | tf_op jit(solution)/shard_map/all_to_all | solution.py:425
  72.3 0.0 copy-start.2
  72.3 1.6 copy-done.2
  73.9 0.9 copy-done.12
  74.8 0.9 copy-done.16
  75.7 0.9 copy-done.19
  76.6 7.7 %goldstein.4 = bf16[8,64,256]{2,1,0:T(8,128)(2,1)S(1)} custom-call(s32[4]{0:T(128)S(1)} %add_convert_fusion.sel, bf16[32,64,512]{2,1,0:T(8,128)(2,1)S(1)} %copy-done, bf16[32,64,512]{2,1,0:T(8,128)(2,1)S(1)} %copy-done.2, bf16[2,8,32,384]{3,2,1,0:T(8,128)(2,1)} %collective-permute-done.one, bf16[2,8,32,384]{3,2,1,0:T(8,128)(2,1)} %collective-permute-done.1.two, ...), custom_call_target="tpu_custom_call" | custom-call | flops 6144000000 | bytes 1048576 | tf_op jit(solution)/shard_map/goldstein/pallas_call | solution.py:206
  84.3 3.4 %all-to-all-done.d_ref = bf16[8,8,32,256]{3,2,1,0:T(8,128)(2,1)S(1)} async-done(((bf16[8,8,32,256]{3,2,1,0:T(8,128)(2,1)}), bf16[8,8,32,256]{3,2,1,0:T(8,128)(2,1)S(1)}, u32[]{:S(2)}, u32[]{:S(2)}) %all-to-all-start) | async-done | bytes 1048608 | tf_op jit(solution)/shard_map/all_to_all | solution.py:425
  87.7 0.9 copy-done.23
  88.6 0.9 copy-done.26
  89.5 0.9 copy-done.29
  90.4 0.9 copy-done.32
  91.3 6.9 %huber.2 = bf16[8,8,40,256]{3,2,1,0:T(8,128)(2,1)} custom-call(bf16[8,8,32,256]{3,2,1,0:T(8,128)(2,1)S(1)} %all-to-all-done.d_ref, bf16[256,256]{1,0:T(8,128)(2,1)S(1)} %copy-done.29, bf16[256,256]{1,0:T(8,128)(2,1)S(1)} %copy-done.32, bf16[320,256]{1,0:T(8,128)(2,1)S(1)} %copy-done.23, bf16[320,256]{1,0:T(8,128)(2,1)S(1)} %copy-done.26), custom_call_target="tpu_custom_call" | custom-call | flops 2617245696 | bytes 2097152 | tf_op jit(solution)/shard_map/huber/pallas_call | solution.py:298
  98.2 4.4 %all-to-all-start.1 = ((bf16[8,8,40,256]{3,2,1,0:T(8,128)(2,1)}), bf16[8,8,40,256]{3,2,1,0:T(8,128)(2,1)}, u32[]{:S(2)}, u32[]{:S(2)}) async-start(bf16[8,8,40,256]{3,2,1,0:T(8,128)(2,1)} %huber.2), calls=%async_computation.1 | async-start | bytes 2621440 | tf_op jit(solution)/shard_map/all_to_all | solution.py:428
  102.7 1.6 copy-done.3
  104.3 1.3 copy-done.10
  105.5 0.9 copy-done.17
  106.4 0.9 copy-done.20
  107.3 20.7 %goldstein.7 = bf16[24,64,256]{2,1,0:T(8,128)(2,1)S(1)} custom-call(s32[4]{0:T(128)S(1)} %add_convert_fusion.sel, bf16[32,64,512]{2,1,0:T(8,128)(2,1)S(1)} %copy-done, bf16[32,64,512]{2,1,0:T(8,128)(2,1)S(1)} %copy-done.3, bf16[2,24,32,384]{3,2,1,0:T(8,128)(2,1)} %collective-permute-done.4.one, bf16[2,24,32,384]{3,2,1,0:T(8,128)(2,1)S(1)} %copy-done.10, ...), custom_call_target="tpu_custom_call" | custom-call | flops 18432000000 | bytes 3145728 | tf_op jit(solution)/shard_map/goldstein/pallas_call | solution.py:206
  128.0 0.1 pad_maximum_fusion.2
  128.1 0.6 copy.24
  128.7 19.4 %all_to_all.20.d_ref = bf16[8,8,32,256]{3,2,1,0:T(8,128)(2,1)S(1)} all-to-all(bf16[8,8,32,256]{3,2,1,0:T(8,128)(2,1)S(1)} %bitcast.39), channel_id=1, replica_groups=mesh['ifg'=8,'row'=4] {'ifg'}, dimensions={0} | all-to-all | bytes 2097152 | tf_op jit(solution)/shard_map/all_to_all | solution.py:425
  148.1 7.0 %huber.3 = bf16[8,8,40,256]{3,2,1,0:T(8,128)(2,1)} custom-call(bf16[8,8,32,256]{3,2,1,0:T(8,128)(2,1)S(1)} %all_to_all.20.d_ref, bf16[256,256]{1,0:T(8,128)(2,1)S(1)} %copy-done.30, bf16[256,256]{1,0:T(8,128)(2,1)S(1)} %copy-done.33, bf16[320,256]{1,0:T(8,128)(2,1)S(1)} %copy-done.24, bf16[320,256]{1,0:T(8,128)(2,1)S(1)} %copy-done.27), custom_call_target="tpu_custom_call" | custom-call | flops 2617245696 | bytes 2097152 | tf_op jit(solution)/shard_map/huber/pallas_call | solution.py:298
  155.1 4.3 %all-to-all-start.3 = ((bf16[8,8,40,256]{3,2,1,0:T(8,128)(2,1)}), bf16[8,8,40,256]{3,2,1,0:T(8,128)(2,1)}, u32[]{:S(2)}, u32[]{:S(2)}) async-start(bf16[8,8,40,256]{3,2,1,0:T(8,128)(2,1)} %huber.3), calls=%async_computation.3 | async-start | bytes 2621440 | tf_op jit(solution)/shard_map/all_to_all | solution.py:428
  159.4 1.6 copy.30
  161.0 0.9 broadcast_select_fusion.7
  161.9 1.6 collective-permute-start.8
  163.5 3.5 %collective-permute-start.6 = (bf16[40,16,256]{2,1,0:T(8,128)(2,1)}, bf16[40,16,256]{2,1,0:T(8,128)(2,1)S(1)}, u32[]{:S(2)}, u32[]{:S(2)}) collective-permute-start(bf16[40,16,256]{2,1,0:T(8,128)(2,1)} %get-tuple-element.35), channel_id=1, source_target_pairs={{0,1},{1,0},{2,3},{3,2},{4,5},{5,4},{6,7},{7,6},{8,9},{9,8},{10,11... | collective-permute-start | bytes 983048 | tf_op jit(solution)/shard_map/ppermute | solution.py:387
  166.9 10.6 %all-to-all-done.3 = bf16[8,8,40,256]{3,2,1,0:T(8,128)(2,1)} async-done(((bf16[8,8,40,256]{3,2,1,0:T(8,128)(2,1)}), bf16[8,8,40,256]{3,2,1,0:T(8,128)(2,1)}, u32[]{:S(2)}, u32[]{:S(2)}) %all-to-all-start.3) | async-done | bytes 1310752 | tf_op jit(solution)/shard_map/all_to_all | solution.py:428
  177.5 1.6 copy.29
  179.2 0.0 copy-start.35
  179.2 0.0 copy-start.4
  179.2 0.0 copy-start.5
  179.2 0.0 copy-start.6
  179.2 0.0 copy-start.7
  179.2 0.9 broadcast_select_fusion.6
  180.1 1.8 collective-permute-start.9
  181.9 3.5 %collective-permute-start.7 = (bf16[40,16,256]{2,1,0:T(8,128)(2,1)}, bf16[40,16,256]{2,1,0:T(8,128)(2,1)}, u32[]{:S(2)}, u32[]{:S(2)}) collective-permute-start(bf16[40,16,256]{2,1,0:T(8,128)(2,1)} %get-tuple-element.33), channel_id=1, source_target_pairs={{0,1},{1,0},{2,3},{3,2},{4,5},{5,4},{6,7},{7,6},{8,9},{9,8},{10,11... | collective-permute-start | bytes 983048 | tf_op jit(solution)/shard_map/ppermute | solution.py:387
  185.3 0.1 select_reduce_fusion
  185.5 0.1 copy.26.refs_9_
  185.6 5.1 %collective-permute-done.7.refs_3_ = bf16[40,16,256]{2,1,0:T(8,128)(2,1)} collective-permute-done((bf16[40,16,256]{2,1,0:T(8,128)(2,1)}, bf16[40,16,256]{2,1,0:T(8,128)(2,1)}, u32[]{:S(2)}, u32[]{:S(2)}) %collective-permute-start.7) | collective-permute-done | bytes 327712 | tf_op jit(solution)/shard_map/ppermute | solution.py:387
  190.7 7.8 %blur.1 = (f32[40,64,512]{2,1,0:T(8,128)}, f32[40,64,512]{2,1,0:T(8,128)}) custom-call(s32[4]{0:T(128)S(1)} %add_convert_fusion.sel, bf16[40,64,256]{2,1,0:T(8,128)(2,1)S(1)} %bitcast.34, bf16[40,64,256]{2,1,0:T(8,128)(2,1)} %bitcast.37, bf16[40,16,256]{2,1,0:T(8,128)(2,1)S(1)} %collective-permute-done.6.refs_2_, ...), custom_call_target="tpu_custom_call" | custom-call | tf_op jit(solution)/shard_map/blur/pallas_call | solution.py:366
  (63 shorter events, 0.1 us)
Async XLA Ops:
  0.6 9.0 %copy-start = (bf16[32,64,512]{2,1,0:T(8,128)(2,1)S(1)}, bf16[32,64,512]{2,1,0:T(8,128)(2,1)}, u32[]{:S(2)}) copy-start(bf16[32,64,512]{2,1,0:T(8,128)(2,1)} %re.7) | copy-start | bytes 6291460
  3.1 30.6 %collective-permute-start.1 = (bf16[2,8,32,384]{3,2,1,0:T(8,128)(2,1)}, bf16[2,8,32,384]{3,2,1,0:T(8,128)(2,1)}, u32[]{:S(2)}, u32[]{:S(2)}) collective-permute-start(bf16[2,8,32,384]{3,2,1,0:T(8,128)(2,1)} %get-tuple-element.38), channel_id=1, source_target_pairs={{0,0},{1,2},{2,1},{3,3},{4,4},{5,6},{6,5},{7,7},{8,8},{9,10},{10,9... | collective-permute-start | bytes 1179656 | tf_op jit(solution)/shard_map/ppermute | solution.py:387
  7.6 26.2 %collective-permute-start = (bf16[2,8,32,384]{3,2,1,0:T(8,128)(2,1)}, bf16[2,8,32,384]{3,2,1,0:T(8,128)(2,1)}, u32[]{:S(2)}, u32[]{:S(2)}) collective-permute-start(bf16[2,8,32,384]{3,2,1,0:T(8,128)(2,1)} %get-tuple-element.39), channel_id=1, source_target_pairs={{0,1},{1,0},{2,3},{3,2},{4,5},{5,4},{6,7},{7,6},{8,9},{9,8},{10,11... | collective-permute-start | bytes 1179656 | tf_op jit(solution)/shard_map/ppermute | solution.py:387
  13.0 28.5 %collective-permute-start.5 = (bf16[2,24,32,384]{3,2,1,0:T(8,128)(2,1)}, bf16[2,24,32,384]{3,2,1,0:T(8,128)(2,1)S(1)}, u32[]{:S(2)}, u32[]{:S(2)}) collective-permute-start(bf16[2,24,32,384]{3,2,1,0:T(8,128)(2,1)} %get-tuple-element.30), channel_id=1, source_target_pairs={{0,0},{1,2},{2,1},{3,3},{4,4},{5,6},{6,5},{7,7},{8,8},{9,10},{10,9... | collective-permute-start | bytes 3538952 | tf_op jit(solution)/shard_map/ppermute | solution.py:387
  14.9 31.3 %collective-permute-start.4 = (bf16[2,24,32,384]{3,2,1,0:T(8,128)(2,1)}, bf16[2,24,32,384]{3,2,1,0:T(8,128)(2,1)}, u32[]{:S(2)}, u32[]{:S(2)}) collective-permute-start(bf16[2,24,32,384]{3,2,1,0:T(8,128)(2,1)} %get-tuple-element.31), channel_id=1, source_target_pairs={{0,1},{1,0},{2,3},{3,2},{4,5},{5,4},{6,7},{7,6},{8,9},{9,8},{10,11... | collective-permute-start | bytes 3538952 | tf_op jit(solution)/shard_map/ppermute | solution.py:387
  20.3 6.6 %copy-start.8 = (s32[256,2]{0,1:T(2,128)S(1)}, s32[256,2]{0,1:T(2,128)}, u32[]{:S(2)}) copy-start(s32[256,2]{0,1:T(2,128)} %param.15) | copy-start | bytes 6148
  21.5 50.7 %collective-permute-start.3 = (bf16[2,32,32,128]{3,2,1,0:T(8,128)(2,1)}, bf16[2,32,32,128]{3,2,1,0:T(8,128)(2,1)}, u32[]{:S(2)}, u32[]{:S(2)}) collective-permute-start(bf16[2,32,32,128]{3,2,1,0:T(8,128)(2,1)} %get-tuple-element.36), channel_id=1, source_target_pairs={{0,0},{1,2},{2,1},{3,3},{4,4},{5,6},{6,5},{7,7},{8,8},{9,10},{10,9... | collective-permute-start | bytes 1572872 | tf_op jit(solution)/shard_map/ppermute | solution.py:387
  27.1 6.6 %copy-start.1 = (bf16[32,64,512]{2,1,0:T(8,128)(2,1)S(1)}, bf16[32,64,512]{2,1,0:T(8,128)(2,1)}, u32[]{:S(2)}) copy-start(bf16[32,64,512]{2,1,0:T(8,128)(2,1)} %im.7) | copy-start | bytes 6291460
  27.1 6.6 %copy-start.11 = (bf16[384,256]{1,0:T(8,128)(2,1)S(1)}, bf16[384,256]{1,0:T(8,128)(2,1)}, u32[]{:S(2)}) copy-start(bf16[384,256]{1,0:T(8,128)(2,1)} %constant.63.clone.refs_3_.refs_1_) | copy-start | bytes 589828
  27.1 6.6 %copy-start.14 = (bf16[256,256]{1,0:T(8,128)(2,1)S(1)}, bf16[256,256]{1,0:T(8,128)(2,1)}, u32[]{:S(2)}) copy-start(bf16[256,256]{1,0:T(8,128)(2,1)} %constant.65.clone.refs_5_.refs_3_) | copy-start | bytes 393220
  27.1 6.6 %copy-start.15 = (bf16[256,256]{1,0:T(8,128)(2,1)S(1)}, bf16[256,256]{1,0:T(8,128)(2,1)}, u32[]{:S(2)}) copy-start(bf16[256,256]{1,0:T(8,128)(2,1)} %constant.62.clone.refs_2_.refs_0_) | copy-start | bytes 393220
  27.1 6.6 %copy-start.18 = (bf16[128,384]{1,0:T(8,128)(2,1)S(1)}, bf16[128,384]{1,0:T(8,128)(2,1)}, u32[]{:S(2)}) copy-start(bf16[128,384]{1,0:T(8,128)(2,1)} %constant.64.clone.refs_4_.refs_2_) | copy-start | bytes 294916
  27.2 6.6 %copy-start.21 = (f32[1,256]{1,0:T(1,128)S(1)}, f32[1,256]{1,0:T(1,128)}, u32[]{:S(2)}) copy-start(f32[1,256]{1,0:T(1,128)} %constant.66.clone.refs_6_.refs_4_) | copy-start | bytes 3076
  33.6 7.9 %copy-start.22 = (bf16[320,256]{1,0:T(8,128)(2,1)}, bf16[320,256]{1,0:T(8,128)(2,1)S(1)}, u32[]{:S(2)}) copy-start(bf16[320,256]{1,0:T(8,128)(2,1)S(1)} %get-tuple-element.23.p_hi) | copy-start | bytes 491524
  33.6 7.9 %copy-start.25 = (bf16[320,256]{1,0:T(8,128)(2,1)}, bf16[320,256]{1,0:T(8,128)(2,1)S(1)}, u32[]{:S(2)}) copy-start(bf16[320,256]{1,0:T(8,128)(2,1)S(1)} %get-tuple-element.24.p_lo) | copy-start | bytes 491524
  33.6 7.9 %copy-start.28 = (bf16[256,256]{1,0:T(8,128)(2,1)}, bf16[256,256]{1,0:T(8,128)(2,1)S(1)}, u32[]{:S(2)}) copy-start(bf16[256,256]{1,0:T(8,128)(2,1)S(1)} %get-tuple-element.21.k_hi) | copy-start | bytes 393220
  33.6 7.9 %copy-start.31 = (bf16[256,256]{1,0:T(8,128)(2,1)}, bf16[256,256]{1,0:T(8,128)(2,1)S(1)}, u32[]{:S(2)}) copy-start(bf16[256,256]{1,0:T(8,128)(2,1)S(1)} %get-tuple-element.22.k_lo) | copy-start | bytes 393220
  33.7 38.6 %collective-permute-start.2 = (bf16[2,32,32,128]{3,2,1,0:T(8,128)(2,1)}, bf16[2,32,32,128]{3,2,1,0:T(8,128)(2,1)}, u32[]{:S(2)}, u32[]{:S(2)}) collective-permute-start(bf16[2,32,32,128]{3,2,1,0:T(8,128)(2,1)} %get-tuple-element.37), channel_id=1, source_target_pairs={{0,1},{1,0},{2,3},{3,2},{4,5},{5,4},{6,7},{7,6},{8,9},{9,8},{10,11... | collective-permute-start | bytes 1572872 | tf_op jit(solution)/shard_map/ppermute | solution.py:387
  41.5 25.4 %copy-start.9 = (bf16[2,24,32,384]{3,2,1,0:T(8,128)(2,1)}, bf16[2,24,32,384]{3,2,1,0:T(8,128)(2,1)S(1)}, u32[]{:S(2)}) copy-start(bf16[2,24,32,384]{3,2,1,0:T(8,128)(2,1)S(1)} %collective-permute-done.5.two) | copy-start | bytes 3538948
  68.6 19.1 %all-to-all-start = ((bf16[8,8,32,256]{3,2,1,0:T(8,128)(2,1)}), bf16[8,8,32,256]{3,2,1,0:T(8,128)(2,1)S(1)}, u32[]{:S(2)}, u32[]{:S(2)}) async-start(bf16[8,8,32,256]{3,2,1,0:T(8,128)(2,1)} %bitcast.38), calls=%async_computation | async-start | bytes 2097152 | tf_op jit(solution)/shard_map/all_to_all | solution.py:425
  72.3 1.6 copy-start.2
  73.9 0.9 copy-start.12
  74.8 0.9 copy-start.16
  75.7 0.9 copy-start.19
  87.7 0.9 copy-start.23
  88.6 0.9 copy-start.26
  89.5 0.9 copy-start.29
  90.4 0.9 copy-start.32
  98.2 4.4 %copy-start.13 = (bf16[384,256]{1,0:T(8,128)(2,1)S(1)}, bf16[384,256]{1,0:T(8,128)(2,1)}, u32[]{:S(2)}) copy-start(bf16[384,256]{1,0:T(8,128)(2,1)} %constant.63.clone.refs_3_.refs_1_) | copy-start | bytes 589828
  98.2 29.8 %all-to-all-start.1 = ((bf16[8,8,40,256]{3,2,1,0:T(8,128)(2,1)}), bf16[8,8,40,256]{3,2,1,0:T(8,128)(2,1)}, u32[]{:S(2)}, u32[]{:S(2)}) async-start(bf16[8,8,40,256]{3,2,1,0:T(8,128)(2,1)} %huber.2), calls=%async_computation.1 | async-start | bytes 2621440 | tf_op jit(solution)/shard_map/all_to_all | solution.py:428
  102.7 1.6 copy-start.3
  104.3 1.3 copy-start.10
  105.5 0.9 copy-start.17
  106.4 0.9 copy-start.20
  128.7 19.4 %copy-start.24 = (bf16[320,256]{1,0:T(8,128)(2,1)S(1)}, bf16[320,256]{1,0:T(8,128)(2,1)}, u32[]{:S(2)}) copy-start(bf16[320,256]{1,0:T(8,128)(2,1)} %copy-done.22) | copy-start | bytes 491524
  128.7 19.4 %copy-start.27 = (bf16[320,256]{1,0:T(8,128)(2,1)S(1)}, bf16[320,256]{1,0:T(8,128)(2,1)}, u32[]{:S(2)}) copy-start(bf16[320,256]{1,0:T(8,128)(2,1)} %copy-done.25) | copy-start | bytes 491524
  128.7 19.4 %copy-start.30 = (bf16[256,256]{1,0:T(8,128)(2,1)S(1)}, bf16[256,256]{1,0:T(8,128)(2,1)}, u32[]{:S(2)}) copy-start(bf16[256,256]{1,0:T(8,128)(2,1)} %copy-done.28) | copy-start | bytes 393220
  128.7 19.4 %copy-start.33 = (bf16[256,256]{1,0:T(8,128)(2,1)S(1)}, bf16[256,256]{1,0:T(8,128)(2,1)}, u32[]{:S(2)}) copy-start(bf16[256,256]{1,0:T(8,128)(2,1)} %copy-done.31) | copy-start | bytes 393220
  155.1 22.5 %all-to-all-start.3 = ((bf16[8,8,40,256]{3,2,1,0:T(8,128)(2,1)}), bf16[8,8,40,256]{3,2,1,0:T(8,128)(2,1)}, u32[]{:S(2)}, u32[]{:S(2)}) async-start(bf16[8,8,40,256]{3,2,1,0:T(8,128)(2,1)} %huber.3), calls=%async_computation.3 | async-start | bytes 2621440 | tf_op jit(solution)/shard_map/all_to_all | solution.py:428
  161.9 23.7 %collective-permute-start.8 = (bf16[40,16,256]{2,1,0:T(8,128)(2,1)}, bf16[40,16,256]{2,1,0:T(8,128)(2,1)S(1)}, u32[]{:S(2)}, u32[]{:S(2)}) collective-permute-start(bf16[40,16,256]{2,1,0:T(8,128)(2,1)} %get-tuple-element.34), channel_id=1, source_target_pairs={{0,0},{1,2},{2,1},{3,3},{4,4},{5,6},{6,5},{7,7},{8,8},{9,10},{10,9... | collective-permute-start | bytes 983048 | tf_op jit(solution)/shard_map/ppermute | solution.py:387
  163.5 22.1 %collective-permute-start.6 = (bf16[40,16,256]{2,1,0:T(8,128)(2,1)}, bf16[40,16,256]{2,1,0:T(8,128)(2,1)S(1)}, u32[]{:S(2)}, u32[]{:S(2)}) collective-permute-start(bf16[40,16,256]{2,1,0:T(8,128)(2,1)} %get-tuple-element.35), channel_id=1, source_target_pairs={{0,1},{1,0},{2,3},{3,2},{4,5},{5,4},{6,7},{7,6},{8,9},{9,8},{10,11... | collective-permute-start | bytes 983048 | tf_op jit(solution)/shard_map/ppermute | solution.py:387
  179.2 6.3 %copy-start.34 = (bf16[40,8,8,256]{3,2,1,0:T(8,128)(2,1)}, bf16[40,8,8,256]{3,2,1,0:T(8,128)(2,1)S(1)}, u32[]{:S(2)}) copy-start(bf16[40,8,8,256]{3,2,1,0:T(8,128)(2,1)S(1)} %copy.29) | copy-start | bytes 3932164
  179.2 6.2 %copy-start.35 = (f32[64,96]{1,0:T(8,128)S(1)}, f32[64,96]{1,0:T(8,128)}, u32[]{:S(2)}) copy-start(f32[64,96]{1,0:T(8,128)} %constant.68.clone) | copy-start | bytes 73732
  179.2 11.5 %copy-start.4 = (bf16[512,512]{1,0:T(8,128)(2,1)S(1)}, bf16[512,512]{1,0:T(8,128)(2,1)}, u32[]{:S(2)}) copy-start(bf16[512,512]{1,0:T(8,128)(2,1)} %constant.70.clone.refs_8_) | copy-start | bytes 1572868
  179.2 11.5 %copy-start.5 = (bf16[512,512]{1,0:T(8,128)(2,1)S(1)}, bf16[512,512]{1,0:T(8,128)(2,1)}, u32[]{:S(2)}) copy-start(bf16[512,512]{1,0:T(8,128)(2,1)} %constant.69.clone.refs_7_) | copy-start | bytes 1572868
  179.2 11.5 %copy-start.6 = (bf16[128,96]{1,0:T(8,128)(2,1)S(1)}, bf16[128,96]{1,0:T(8,128)(2,1)}, u32[]{:S(2)}) copy-start(bf16[128,96]{1,0:T(8,128)(2,1)} %constant.67.clone.refs_6_) | copy-start | bytes 73732
  179.2 11.5 %copy-start.7 = (f32[1,512]{1,0:T(1,128)S(1)}, f32[1,512]{1,0:T(1,128)}, u32[]{:S(2)}) copy-start(f32[1,512]{1,0:T(1,128)} %constant.72.refs_10_) | copy-start | bytes 6148
  180.1 5.5 %collective-permute-start.9 = (bf16[40,16,256]{2,1,0:T(8,128)(2,1)}, bf16[40,16,256]{2,1,0:T(8,128)(2,1)S(1)}, u32[]{:S(2)}, u32[]{:S(2)}) collective-permute-start(bf16[40,16,256]{2,1,0:T(8,128)(2,1)} %get-tuple-element.32), channel_id=1, source_target_pairs={{0,0},{1,2},{2,1},{3,3},{4,4},{5,6},{6,5},{7,7},{8,8},{9,10},{10,9... | collective-permute-start | bytes 983048 | tf_op jit(solution)/shard_map/ppermute | solution.py:387
  181.9 8.8 %collective-permute-start.7 = (bf16[40,16,256]{2,1,0:T(8,128)(2,1)}, bf16[40,16,256]{2,1,0:T(8,128)(2,1)}, u32[]{:S(2)}, u32[]{:S(2)}) collective-permute-start(bf16[40,16,256]{2,1,0:T(8,128)(2,1)} %get-tuple-element.33), channel_id=1, source_target_pairs={{0,1},{1,0},{2,3},{3,2},{4,5},{5,4},{6,7},{7,6},{8,9},{9,8},{10,11... | collective-permute-start | bytes 983048 | tf_op jit(solution)/shard_map/ppermute | solution.py:387
